TPU v7x, 768 devices: a whole 4x8x12 slice. The times are simulated.
768 devices in a mesh: tile: 96 (over y_lo, x, z), chan: 8 (over y_hi, core).
Axes of the slice: x: 4, y: 8 (y_hi: 4, y_lo: 2; y = y_hi * 2 + y_lo), z: 12, core: 2. Of those that a mesh axis runs over, the one named last changes fastest.
Arguments:
- inputs: bfloat16 [96, 256, 1024], P('tile', 'chan'), may hold values from -6 to 6
- grad_out: bfloat16 [96, 256, 1024], P('tile', 'chan'), may hold values from -6 to 6
- kernel: bfloat16 [25, 256], P(None, 'chan'), may hold values from -1.25 to 1.25
- w_in: bfloat16 [256, 1024], replicated, may hold values from -0.375 to 0.375
- w_out: bfloat16 [1024, 256], replicated, may hold values from -0.1875 to 0.1875
- neighbours: int32 [96, 8], replicated, may hold values from 0 to 95, as said below
- rotations: int32 [96, 8], replicated, may hold values from 0 to 3, as said below
Outputs:
- outputs: bfloat16 [96, 256, 1024], P('tile', 'chan')
- grad_in: bfloat16 [96, 256, 1024], P('tile', 'chan')
- grad_w_in: float32 [256, 1024], replicated
- grad_w_out: float32 [1024, 256], replicated
- grad_kernel: float32 [25, 256], replicated
Inputs may be any that keep to these rules, and one draw needn't show every extreme that they name: neighbours[t, d] is the tile that borders tile t in direction d; for every tile t and direction d exactly one tile s has neighbours[s, d] = t, namely s = neighbours[t, 7 - d]. rotations[t, d] is the number of quarter turns that brings the bordering tile into tile t's frame.
All inputs are finite; a program needn't handle non-finite values.
Results may differ from a plain program's by a relative error of at most 0.006.
Values may be sent and summed in bfloat16 or wider, within the bound.
A program may use at most 64 MiB of HBM per device.

v0:
```python
import math

import jax
import jax.numpy as jnp
from jax import lax
from jax.sharding import PartitionSpec as P

KSIZE = 5


offsets = ((-1, -1), (-1, 0), (-1, 1), (0, -1), (0, 1), (1, -1), (1, 0), (1, 1))


def source_span(step_dir, edge_len, halo_width):
    if step_dir < 0:
        return (edge_len - halo_width, edge_len)
    if step_dir > 0:
        return (0, halo_width)
    return (0, edge_len)


def target_span(step_dir, edge_len, halo_width):
    if step_dir < 0:
        return (0, halo_width)
    if step_dir > 0:
        return (halo_width + edge_len, edge_len + 2 * halo_width)
    return (halo_width, halo_width + edge_len)


def turn_span(rows_span, cols_span, quarter, edge_len):
    for repeat in range(quarter):
        rows_span, cols_span = (cols_span, (edge_len - rows_span[1], edge_len - rows_span[0]))
    return (tuple(rows_span), tuple(cols_span))


def band_shape(band_pick, channels, edge_len, halo_width):
    if band_pick < 2:
        return (channels, halo_width, edge_len)
    return (channels, edge_len, halo_width)


def band_anchor(band_pick, edge_len, halo_width):
    row_base = edge_len - halo_width if band_pick == 1 else 0
    col_base = edge_len - halo_width if band_pick == 3 else 0
    return (row_base, col_base)


def band_block(flat_rims, channels, edge_len, halo_width, rows_span, cols_span):
    band_len = channels * halo_width * edge_len
    if rows_span[1] <= halo_width:
        band_pick = 0
    elif rows_span[0] >= edge_len - halo_width:
        band_pick = 1
    elif cols_span[1] <= halo_width:
        band_pick = 2
    else:
        band_pick = 3
    strip_data = flat_rims[band_pick * band_len : (band_pick + 1) * band_len].reshape(
        band_shape(band_pick, channels, edge_len, halo_width)
    )
    row_base, col_base = band_anchor(band_pick, edge_len, halo_width)
    return strip_data[
        :,
        rows_span[0] - row_base : rows_span[1] - row_base,
        cols_span[0] - col_base : cols_span[1] - col_base,
    ]


def depthwise(padded, kernel, edge_len):
    result = jnp.zeros(padded.shape[:-2] + (edge_len, edge_len), jnp.float32)
    for tap_row in range(KSIZE):
        for tap_col in range(KSIZE):
            weight = kernel[tap_row * KSIZE + tap_col].astype(jnp.float32)[:, None, None]
            result = result + weight * padded[
                ..., tap_row : tap_row + edge_len, tap_col : tap_col + edge_len
            ].astype(jnp.float32)
    return result


def spread(grads, kernel, row_span, col_span):
    margin = KSIZE - 1
    widths = [(0, 0)] * (grads.ndim - 2) + [(margin, margin), (margin, margin)]
    widened = jnp.pad(grads, widths)
    result = jnp.zeros(
        grads.shape[:-2] + (row_span[1] - row_span[0], col_span[1] - col_span[0]), jnp.float32
    )
    for tap_row in range(KSIZE):
        for tap_col in range(KSIZE):
            weight = kernel[tap_row * KSIZE + tap_col].astype(jnp.float32)[:, None, None]
            result = (
                result
                + weight
                * widened[
                    ...,
                    row_span[0] + margin - tap_row : row_span[1] + margin - tap_row,
                    col_span[0] + margin - tap_col : col_span[1] + margin - tap_col,
                ]
            )
    return result


def kernel_grads(grad_tiles, padded, edge_len, sum_axes):
    columns = []
    for tap_row in range(KSIZE):
        for tap_col in range(KSIZE):
            window = padded[..., tap_row : tap_row + edge_len, tap_col : tap_col + edge_len].astype(
                jnp.float32
            )
            columns.append(jnp.sum(grad_tiles * window, axis=sum_axes))
    return jnp.stack(columns, axis=0)


def gelu_slope(values):
    cumul = 0.5 * (1.0 + lax.erf(values * 0.7071067811865476))
    return cumul + values * jnp.exp(-0.5 * values * values) * 0.3989422804014327


def pack_rims(images, halo_width):
    edge_len = images.shape[-1]
    pieces_list = [
        images[:, :halo_width, :],
        images[:, edge_len - halo_width :, :],
        images[:, :, :halo_width],
        images[:, :, edge_len - halo_width :],
    ]
    return jnp.concatenate([region.reshape(-1) for region in pieces_list])


def add_turned(accum, pieces_list, edge_len):
    totals = {}
    for rows_span, cols_span, quarter, region in pieces_list:
        target_box = turn_span(rows_span, cols_span, quarter, edge_len)
        turned_part = jnp.rot90(region, -quarter, axes=(1, 2))
        if target_box in totals:
            totals[target_box] = totals[target_box] + turned_part
        else:
            totals[target_box] = turned_part
    for target_box in totals:
        accum = accum.at[
            :, target_box[0][0] : target_box[0][1], target_box[1][0] : target_box[1][1]
        ].add(totals[target_box])
    return accum


def fold_rims(rim_rows, combine, start_value):
    return combine(start_value, lax.all_gather(rim_rows, "tile", axis=0, tiled=True), jnp.int32(0))


def hit_table(neighbours, rotations, my_index, direction):
    bordered = neighbours[:, direction]
    turn_codes = rotations[:, direction]
    matches = (bordered == my_index)[:, None] & (
        turn_codes[:, None] == jnp.arange(4, dtype=jnp.int32)[None, :]
    )
    return matches.astype(jnp.float32)


def body(inputs, grad_out, kernel, w_in, w_out, neighbours, rotations):
    channels = inputs.shape[1]
    pixels = inputs.shape[2]
    edge_len = math.isqrt(pixels)
    halo_width = KSIZE // 2
    ext_len = edge_len + 2 * halo_width
    groups = lax.axis_size("chan")
    tile_count = lax.axis_size("tile")
    my_index = lax.axis_index("tile")
    chan_index = lax.axis_index("chan")
    full_channels = w_in.shape[0]
    grad_scale = (tile_count * pixels) ** (-0.5)
    own_tile = inputs.reshape(channels, edge_len, edge_len)
    own_row = lax.dynamic_index_in_dim(neighbours, my_index, 0, keepdims=False)
    own_turns = lax.dynamic_index_in_dim(rotations, my_index, 0, keepdims=False)
    rim_len = 4 * halo_width * edge_len * channels

    def pick_rims(selected, shard_rows, first_row):
        num_rows = shard_rows.shape[0]
        result = []
        for direction in range(8):
            position = own_row[direction]
            present = (position >= 0) & (position < num_rows)
            candidate = lax.dynamic_index_in_dim(
                shard_rows, jnp.clip(position, 0, num_rows - 1), 0, keepdims=False
            )
            result.append(jnp.where(present, candidate, selected[direction]))
        return tuple(result)

    empty_rims = tuple((jnp.zeros((rim_len,), jnp.bfloat16) for direction in range(8)))
    selected = fold_rims(pack_rims(own_tile, halo_width)[None, :], pick_rims, empty_rims)
    padded = jnp.zeros((channels, ext_len, ext_len), jnp.bfloat16)
    padded = padded.at[
        :, halo_width : halo_width + edge_len, halo_width : halo_width + edge_len
    ].set(own_tile)
    for direction, (step_row, step_col) in enumerate(offsets):
        src_rows = source_span(step_row, edge_len, halo_width)
        src_cols = source_span(step_col, edge_len, halo_width)
        dst_rows = target_span(step_row, edge_len, halo_width)
        dst_cols = target_span(step_col, edge_len, halo_width)
        candidates = []
        for quarter in range(4):
            from_rows, from_cols = turn_span(src_rows, src_cols, quarter, edge_len)
            block_part = band_block(
                selected[direction], channels, edge_len, halo_width, from_rows, from_cols
            )
            candidates.append(jnp.rot90(block_part, quarter, axes=(1, 2)))
        chosen = candidates[0]
        for quarter in range(1, 4):
            chosen = jnp.where(own_turns[direction] == quarter, candidates[quarter], chosen)
        padded = padded.at[:, dst_rows[0] : dst_rows[1], dst_cols[0] : dst_cols[1]].set(chosen)
    hidden = depthwise(padded, kernel, edge_len).astype(jnp.bfloat16)
    arrived = (
        lax.all_to_all(
            hidden.reshape(channels, groups, pixels // groups),
            "chan",
            split_axis=1,
            concat_axis=0,
            tiled=True,
        ),
        lax.all_to_all(
            grad_out.reshape(channels, groups, pixels // groups),
            "chan",
            split_axis=1,
            concat_axis=0,
            tiled=True,
        ),
    )
    features = arrived[0].reshape(full_channels, pixels // groups)
    cotangent = arrived[1].reshape(full_channels, pixels // groups)
    pre_act = lax.dot_general(
        w_in, features, (((0,), (0,)), ((), ())), preferred_element_type=jnp.float32
    )
    activated = jax.nn.gelu(pre_act, approximate=False).astype(jnp.bfloat16)
    branch_out = lax.dot_general(
        w_out, activated, (((0,), (0,)), ((), ())), preferred_element_type=jnp.float32
    ).astype(jnp.bfloat16)
    grad_act = jnp.dot(w_out, cotangent, preferred_element_type=jnp.float32)
    grad_pre = (grad_act * gelu_slope(pre_act)).astype(jnp.bfloat16)
    grad_feat = jnp.dot(w_in, grad_pre, preferred_element_type=jnp.float32).astype(jnp.bfloat16)
    part_in = lax.dot_general(
        features, grad_pre, (((1,), (1,)), ((), ())), preferred_element_type=jnp.float32
    )
    part_out = lax.dot_general(
        activated, cotangent, (((1,), (1,)), ((), ())), preferred_element_type=jnp.float32
    )
    returned = (
        lax.all_to_all(branch_out[:, None, :], "chan", split_axis=0, concat_axis=1, tiled=True),
        lax.all_to_all(grad_feat[:, None, :], "chan", split_axis=0, concat_axis=1, tiled=True),
    )
    outputs = (
        inputs.astype(jnp.float32) + returned[0].reshape(1, channels, pixels).astype(jnp.float32)
    ).astype(jnp.bfloat16)
    grad_hidden = returned[1].reshape(channels, edge_len, edge_len)
    grad_tile = grad_hidden.astype(jnp.float32)
    grad_padded = spread(grad_tile, kernel, (0, ext_len), (0, ext_len))
    local_kernel = kernel_grads(grad_tile, padded, edge_len, (1, 2))
    accum = grad_out.reshape(channels, edge_len, edge_len).astype(jnp.float32)
    accum = (
        accum
        + grad_padded[:, halo_width : halo_width + edge_len, halo_width : halo_width + edge_len]
    )
    border_pieces = []
    regions_out = []
    region_starts = [0]
    for direction, (step_row, step_col) in enumerate(offsets):
        dst_rows = target_span(step_row, edge_len, halo_width)
        dst_cols = target_span(step_col, edge_len, halo_width)
        region_vec = grad_padded[:, dst_rows[0] : dst_rows[1], dst_cols[0] : dst_cols[1]].reshape(
            -1
        )
        regions_out.append(region_vec)
        region_starts.append(region_starts[-1] + region_vec.shape[0])
    outgoing = jnp.concatenate(regions_out)[None, :]
    start_sums = tuple(
        (
            jnp.zeros((4, region_starts[direction + 1] - region_starts[direction]), jnp.float32)
            for direction in range(8)
        )
    )
    shard_rows = lax.all_gather(outgoing.astype(jnp.bfloat16), "tile", axis=0, tiled=True).astype(
        jnp.float32
    )
    num_rows = shard_rows.shape[0]
    result = []
    for gather_direction in range(8):
        hit_mask = hit_table(neighbours, rotations, my_index, gather_direction)
        gather_region = shard_rows[
            :, region_starts[gather_direction] : region_starts[gather_direction + 1]
        ]
        result.append(
            start_sums[gather_direction]
            + jnp.einsum("kr,kn->rn", hit_mask, gather_region, precision=lax.Precision.HIGHEST)
        )
    received = tuple(result)
    for direction, (step_row, step_col) in enumerate(offsets):
        src_rows = source_span(step_row, edge_len, halo_width)
        src_cols = source_span(step_col, edge_len, halo_width)
        for quarter in range(4):
            region = received[direction][quarter].reshape(
                channels, src_rows[1] - src_rows[0], src_cols[1] - src_cols[0]
            )
            border_pieces.append((src_rows, src_cols, quarter, region))
    accum = add_turned(accum, border_pieces, edge_len)
    full_kernel = lax.dynamic_update_slice(
        jnp.zeros((KSIZE * KSIZE, full_channels), jnp.float32),
        local_kernel,
        (jnp.zeros((), jnp.int32), chan_index * channels),
    )
    summed = lax.psum((part_in, part_out, full_kernel), ("tile", "chan"))
    grad_in = accum.astype(jnp.bfloat16).reshape(1, channels, pixels)
    return (
        outputs,
        grad_in,
        summed[0] * grad_scale,
        summed[1] * grad_scale,
        summed[2] * grad_scale,
    )


def solution(mesh):
    return jax.shard_map(
        body,
        mesh=mesh,
        in_specs=(
            P("tile", "chan", None),
            P("tile", "chan", None),
            P(None, "chan"),
            P(),
            P(),
            P(),
            P(),
        ),
        out_specs=(P("tile", "chan", None), P("tile", "chan", None), P(), P(), P()),
        check_vma=False,
    )
```

profile of v0, /device:TPU:16, one launch (start us, length us, event | category | flops | bytes accessed | tf_op | source)
XLA Modules:
  0.0 1601.3 jit_solution(17148832243587428690)
XLA Ops:
  7.3 1.1 reshape.1233
  9.4 0.6 pad_maximum_fusion
  42.3 0.7 fusion.201
  43.0 0.6 fusion.200
  43.6 0.8 and_reduce_fusion.2
  44.4 0.8 and_reduce_fusion
  45.2 0.7 bitcast_convert_fusion.24
  45.9 422.0 %all-gather.5.cloned.1.call-done = bf16[786432]{0:T(1024)(128)(2,1)} async-done(((bf16[8192]{0:T(1024)(128)(2,1)}), bf16[786432]{0:T(1024)(128)(2,1)}) %all-gather.5.cloned.1.call-update) | async-done | bytes 1572880 | tf_op jit(solution)/shard_map/all_gather | solution.py:146
  467.8 2.5 reshape.1279
  470.4 0.6 broadcast_select_fusion.1
  482.0 1.1 scatter.31
  483.1 2.0 broadcast_select_fusion.24
  485.2 11.0 scatter.34
  496.2 2.1 broadcast_select_fusion.20
  498.4 11.1 scatter.35
  513.3 3.9 scatter.36
  517.3 13.1 scatter.39
  530.5 1.1 scatter.40
  531.6 9.8 scatter.41
  541.4 9.8 scatter.44
  551.4 3.2 fusion.117
  554.8 0.6 copy.137
  555.5 6.3 all-to-all-start
  561.8 0.6 copy.141
  562.5 5.0 all-to-all-done
  567.5 6.2 all-to-all-start.2
  573.7 1.3 fusion.103
  574.9 5.2 all-to-all-done.2
  580.8 1.3 fusion.202
  582.6 0.7 reduce.221
  583.4 0.7 reshape.1466
  584.0 5.2 all-to-all-start.3
  589.2 1.3 fusion.203
  590.6 5.1 all-to-all-done.3
  596.0 4.7 fusion.186
  603.6 0.7 reduce.220
  604.4 0.7 reshape.1464
  605.1 5.4 all-to-all-start.1
  611.2 5.7 all-to-all-done.1
  617.2 0.7 copy.162
  617.9 1.2 fusion.82
  619.1 3.7 fusion.100
  623.3 100.3 %psum.23 = f32[25,256]{1,0:T(8,128)S(1)} all-reduce(f32[25,256]{1,0:T(8,128)S(1)} %dynamic_update_slice.3), channel_id=1, replica_groups=mesh['tile'=96,'chan'=8] {'tile','chan'}, use_global_device_ids=true, to_apply=%region_30.31 | all-reduce | flops 6400 | bytes 51200 | tf_op jit(solution)/shard_map/psum | solution.py:307
  723.6 0.6 broadcast_multiply_fusion.2
  724.4 351.4 %all-reduce.5.cloned.1.call-done = (f32[256,1024]{1,0:T(8,128)}, f32[1024,256]{1,0:T(8,128)}) async-done(((f32[256,1024]{1,0:T(8,128)}, f32[1024,256]{1,0:T(8,128)}), (f32[256,1024]{1,0:T(8,128)}, f32[1024,256]{1,0:T(8,128)})) %all-reduce.5.cloned.1.call-update) | async-done | bytes 2097168 | tf_op jit(solution)/shard_map/psum | solution.py:307
  1075.8 2.4 broadcast_multiply_fusion.1
  1078.3 1.1 broadcast_multiply_fusion
  1079.3 451.1 %all-gather.7.cloned.1.call-done = bf16[96,1,8704]{2,1,0:T(2,128)(2,1)} async-done(((bf16[1,1,8704]{2,1,0:T(2,128)(2,1)}), bf16[96,1,8704]{2,1,0:T(2,128)(2,1)}) %all-gather.7.cloned.1.call-update) | async-done | bytes 1671184 | tf_op jit(solution)/shard_map/all_gather | solution.py:278
  1530.4 2.2 copy.180
  1543.3 9.7 scatter-add.26
  1553.1 1.1 scatter-add.29
  1554.3 1.2 scatter-add.30
  1555.5 2.0 add_select_fusion
  1557.4 11.3 scatter-add.31
  1569.0 0.9 rev.237
  1570.1 1.0 rev.235
  1572.9 1.0 rev.242
  1575.2 1.0 rev.236
  1578.0 1.3 reshape_squeeze.118
  1580.2 2.7 slice_add_fusion.1
  1582.8 2.7 scatter-add.35
  1585.6 1.1 slice_add_fusion
  1586.7 6.7 scatter-add.39
  1593.4 0.9 reshape.1248
  (296 shorter events, 40.5 us)
Async XLA Ops:
  7.2 566.5 %copy-start = (bf16[256,1024]{1,0:T(8,128)(2,1)S(1)}, bf16[256,1024]{1,0:T(8,128)(2,1)}, u32[]{:S(2)}) copy-start(bf16[256,1024]{1,0:T(8,128)(2,1)} %param.44) | copy-start | bytes 1572868
  7.2 36.4 %copy-start.33 = (s32[3]{0:T(128)S(1)}, s32[3]{0:T(128)}, u32[]{:S(2)}) copy-start(s32[3]{0:T(128)} %constant.621.clone.1) | copy-start | bytes 40
  7.2 37.2 %copy-start.31 = (s32[3]{0:T(128)S(1)}, s32[3]{0:T(128)}, u32[]{:S(2)}) copy-start(s32[3]{0:T(128)} %constant.658.clone.1) | copy-start | bytes 40
  7.2 37.2 %copy-start.32 = (s32[3]{0:T(128)S(1)}, s32[3]{0:T(128)}, u32[]{:S(2)}) copy-start(s32[3]{0:T(128)} %constant.624.clone.1) | copy-start | bytes 40
  7.2 2.8 copy-start.9
  7.2 2.8 copy-start.8
  7.2 37.9 %copy-start.7 = (bf16[25,32]{1,0:T(8,128)(2,1)S(1)}, bf16[25,32]{1,0:T(8,128)(2,1)}, u32[]{:S(2)}) copy-start(bf16[25,32]{1,0:T(8,128)(2,1)} %param.43) | copy-start | bytes 4804
  7.2 460.6 %all-gather.5.cloned.1.call-start = ((), (), s32[]{:S(2)}) async-start(), calls=%async_computation.4 | async-start | bytes 1589248 | tf_op jit(solution)/shard_map/all_gather | solution.py:146
  42.3 3.5 copy-start.29
  513.1 38.1 %copy-start.10 = (f32[32]{0:T(128)S(1)}, f32[32]{0:T(128)}, u32[]{:S(2)}) copy-start(f32[32]{0:T(128)} %get-tuple-element.332) | copy-start | bytes 388
  513.1 38.1 %copy-start.11 = (f32[32]{0:T(128)S(1)}, f32[32]{0:T(128)}, u32[]{:S(2)}) copy-start(f32[32]{0:T(128)} %get-tuple-element.333) | copy-start | bytes 388
  513.1 38.1 %copy-start.12 = (f32[32]{0:T(128)S(1)}, f32[32]{0:T(128)}, u32[]{:S(2)}) copy-start(f32[32]{0:T(128)} %get-tuple-element.334) | copy-start | bytes 388
  513.2 38.1 %copy-start.13 = (f32[32]{0:T(128)S(1)}, f32[32]{0:T(128)}, u32[]{:S(2)}) copy-start(f32[32]{0:T(128)} %get-tuple-element.335) | copy-start | bytes 388
  513.2 38.1 %copy-start.14 = (f32[32]{0:T(128)S(1)}, f32[32]{0:T(128)}, u32[]{:S(2)}) copy-start(f32[32]{0:T(128)} %get-tuple-element.336) | copy-start | bytes 388
  513.2 38.1 %copy-start.15 = (f32[32]{0:T(128)S(1)}, f32[32]{0:T(128)}, u32[]{:S(2)}) copy-start(f32[32]{0:T(128)} %get-tuple-element.337) | copy-start | bytes 388
  513.2 38.1 %copy-start.16 = (f32[32]{0:T(128)S(1)}, f32[32]{0:T(128)}, u32[]{:S(2)}) copy-start(f32[32]{0:T(128)} %get-tuple-element.338) | copy-start | bytes 388
  513.2 38.1 %copy-start.17 = (f32[32]{0:T(128)S(1)}, f32[32]{0:T(128)}, u32[]{:S(2)}) copy-start(f32[32]{0:T(128)} %get-tuple-element.339) | copy-start | bytes 388
  513.2 38.1 %copy-start.18 = (f32[32]{0:T(128)S(1)}, f32[32]{0:T(128)}, u32[]{:S(2)}) copy-start(f32[32]{0:T(128)} %get-tuple-element.340) | copy-start | bytes 388
  513.2 38.1 %copy-start.19 = (f32[32]{0:T(128)S(1)}, f32[32]{0:T(128)}, u32[]{:S(2)}) copy-start(f32[32]{0:T(128)} %get-tuple-element.341) | copy-start | bytes 388
  513.2 38.1 %copy-start.20 = (f32[32]{0:T(128)S(1)}, f32[32]{0:T(128)}, u32[]{:S(2)}) copy-start(f32[32]{0:T(128)} %get-tuple-element.342) | copy-start | bytes 388
  513.2 38.1 %copy-start.21 = (f32[32]{0:T(128)S(1)}, f32[32]{0:T(128)}, u32[]{:S(2)}) copy-start(f32[32]{0:T(128)} %get-tuple-element.343) | copy-start | bytes 388
  513.3 38.1 %copy-start.22 = (f32[32]{0:T(128)S(1)}, f32[32]{0:T(128)}, u32[]{:S(2)}) copy-start(f32[32]{0:T(128)} %get-tuple-element.344) | copy-start | bytes 388
  513.3 38.1 %copy-start.23 = (f32[32]{0:T(128)S(1)}, f32[32]{0:T(128)}, u32[]{:S(2)}) copy-start(f32[32]{0:T(128)} %get-tuple-element.345) | copy-start | bytes 388
  513.3 38.1 %copy-start.24 = (f32[32]{0:T(128)S(1)}, f32[32]{0:T(128)}, u32[]{:S(2)}) copy-start(f32[32]{0:T(128)} %get-tuple-element.346) | copy-start | bytes 388
  513.3 38.1 %copy-start.25 = (f32[32]{0:T(128)S(1)}, f32[32]{0:T(128)}, u32[]{:S(2)}) copy-start(f32[32]{0:T(128)} %get-tuple-element.347) | copy-start | bytes 388
  513.3 38.1 %copy-start.26 = (f32[32]{0:T(128)S(1)}, f32[32]{0:T(128)}, u32[]{:S(2)}) copy-start(f32[32]{0:T(128)} %get-tuple-element.348) | copy-start | bytes 388
  513.3 38.1 %copy-start.27 = (f32[32]{0:T(128)S(1)}, f32[32]{0:T(128)}, u32[]{:S(2)}) copy-start(f32[32]{0:T(128)} %get-tuple-element.349) | copy-start | bytes 388
  513.3 38.1 %copy-start.28 = (f32[32]{0:T(128)S(1)}, f32[32]{0:T(128)}, u32[]{:S(2)}) copy-start(f32[32]{0:T(128)} %get-tuple-element.350) | copy-start | bytes 388
  551.4 10.4 copy-start.5
  555.5 12.0 all-to-all-start
  567.5 12.7 all-to-all-start.2
  573.7 6.5 copy-start.3
  584.0 11.6 all-to-all-start.3
  589.2 486.6 %all-reduce.5.cloned.1.call-start = ((), (), s32[]{:S(2)}) async-start(), calls=%async_computation.6 | async-start | bytes 4194304 | tf_op jit(solution)/shard_map/psum | solution.py:307
  590.5 939.9 %all-gather.7.cloned.1.call-start = ((), (), s32[]{:S(2)}) async-start(), calls=%async_computation.5 | async-start | bytes 3377152 | tf_op jit(solution)/shard_map/all_gather | solution.py:278
  601.0 9.6 copy-start.30
  602.3 14.8 copy-start.4
  602.7 0.6 copy-start.6
  605.1 11.8 all-to-all-start.1
  1075.8 2.4 copy-start.2
  1580.2 5.4 copy-start.1
Sparse Core Ops, SparseCore 0:
  11.0 456.7 all-gather.4
  596.4 479.3 all-reduce.4
  1078.5 451.8 all-gather.6
where the time goes:
time: 1610 us; the launch traced here: 1600 us
  waiting for transfers between devices  1250 us (78%)
  local copies, waits for them, and re-layouts  146 us (9%)
  blocking collectives  100 us (6%)
  between operations  46.5 us (3%)
  other arithmetic  32.7 us (2%)
  starting transfers between devices  23.2 us (1%)
    all_gather x1, waiting for transfers between devices, body(): lax.all_gather(outgoing.astype(jnp.bfloat16), 'tile', axis=0, tiled=True)  451 us
    all_gather x1, waiting for transfers between devices, fold_rims(): lax.all_gather(rim_rows, 'tile', axis=0, tiled=True)  422 us
    psum x1, waiting for transfers between devices, body(): summed = lax.psum((part_in, part_out, full_kernel), ('tile', 'chan'))  351 us
    psum x1, blocking collectives, body(): summed = lax.psum((part_in, part_out, full_kernel), ('tile', 'chan'))  100 us
    scatter x8, local copies, waits for them, and re-layouts, body(): padded.at[:, dst_rows[0]:dst_rows[1], dst_cols[0]:dst_cols[1]].set(chosen)  60.9 us
    scatter-add x6, local copies, waits for them, and re-layouts, add_turned(): accum = accum.at[:, target_box[0][0]:target_box[0][1], target_box[1][0]:t...  32.6 us
  transfers between devices with their start and end apart: 7, of which 7 were waited for; matrix products, arithmetic and copies ran while one was open for 2% of the time, Pallas kernels for 0%

commit v1 on v0

v1 whole, which is shorter than its diff:
```python
import jax
import jax.numpy as jnp
from jax import lax
from jax.experimental import pallas as pl
from jax.experimental.pallas import tpu as pltpu
from jax.sharding import PartitionSpec as P

NX, NZ, NYL, NYH = 4, 12, 2, 4
NXY = NX * NYL
NY = NYL * NYH
NCHAN = NYH * 2
CH = 32
SIDE = 32
LANES = 128
GROUPS = 8
PADS = SIDE + 4
TAPS = 25
HID = 1024
FULL = 256
SCALE = (NXY * NZ * SIDE * SIDE) ** -0.5
MESH = pl.DeviceIdType.MESH
F32, BF16, I32 = jnp.float32, jnp.bfloat16, jnp.int32

BASE = (0, 0, 0, 3, 1, 2, 2, 2)
EDGE_DIRS = (1, 3, 4, 6)
CORNER_DIRS = (0, 2, 5, 7)

VMEM = pl.BlockSpec(memory_space=pltpu.VMEM)
SMEM = pl.BlockSpec(memory_space=pltpu.SMEM)


def iota(shape, axis):
    return lax.broadcasted_iota(I32, shape, axis)


def roll(values, shift):
    return pltpu.roll(values, shift % LANES, 1)


def dot(a, b, contract=((1,), (0,)), precision=None):
    return lax.dot_general(a, b, (contract, ((), ())), preferred_element_type=F32, precision=precision)


def turned(q, i, j):
    q0, q1, q2, q3 = [(q == k).astype(I32) for k in range(4)]
    rows = q0 * i + q1 * j + q2 * (31 - i) + q3 * (31 - j)
    cols = q0 * j + q1 * (31 - i) + q2 * (31 - j) + q3 * i
    return rows, cols


def fold(wide):
    low = iota((16, LANES), 1) < 64
    return jnp.where(low, wide[:16], roll(wide[16:], 64))


def unfold(tile):
    tile = tile.astype(F32)
    return jnp.concatenate([tile, roll(tile, 64)], axis=0).astype(BF16)


def spread_taps(k_ref, kb):
    taps = k_ref[...].astype(F32)
    eye = iota((CH, CH), 0) == iota((CH, CH), 1)
    ones = jnp.ones((CH, LANES), BF16)
    for tap in range(TAPS):
        row = jnp.broadcast_to(taps[tap : tap + 1, :], (CH, CH))
        kb[tap] = dot(jnp.where(eye, row, 0.0).astype(BF16), ones)


def rim_kernel(x_ref, o_ref):
    p = iota((1024, 256), 0)
    n = iota((1, 256), 1)
    e, line, i = n >> 6, (n >> 5) & 1, n & 31
    px = jnp.where(e == 0, (30 + line) * 32 + i, 0)
    px = jnp.where(e == 1, i * 32 + line, px)
    px = jnp.where(e == 2, line * 32 + i, px)
    px = jnp.where(e == 3, i * 32 + 30 + line, px)
    rims = dot(x_ref[...], jnp.where(p == px, 1.0, 0.0).astype(BF16))
    low = iota((16, LANES), 1) < 64
    for pair in range(2):
        half = rims[:, LANES * pair : LANES * (pair + 1)]
        upper, lower = half[:16], half[16:]
        o_ref[2 * pair] = jnp.where(low, upper, roll(lower, 64)).astype(BF16)
        o_ref[2 * pair + 1] = jnp.where(low, roll(upper, 64), lower).astype(BF16)


def conv_kernel(rot_ref, x_ref, sel_ref, k_ref, hid_ref, pad_ref, pb, kb):
    me = lax.axis_index("tile")
    spread_taps(k_ref, kb)

    def block(d, i, j, valid):
        q = rot_ref[me, d]
        si, sj = turned(q, i, j)
        e = (q + BASE[d]) & 3
        along = (e & 1) * si + (1 - (e & 1)) * sj
        line = (1 - (e & 1)) * (si - 30 * (e == 0).astype(I32)) + (e & 1) * (sj - 30 * (e == 3).astype(I32))
        lane = jnp.where(valid, line * 32 + along, -1)
        pick = jnp.where(iota((LANES, lane.shape[1]), 0) == lane, 1.0, 0.0).astype(BF16)
        return dot(unfold(sel_ref[d]), pick)

    n = iota((1, 256), 1)
    a, lane = n >> 7, n & 127
    rows = []
    for first, dirs in ((30, (0, 1, 2)), (0, (5, 6, 7))):
        i = first + a
        rows.append(
            block(dirs[0], i, 30 + lane, lane < 2)
            + block(dirs[1], i, lane - 2, (lane >= 2) & (lane < 34))
            + block(dirs[2], i, lane - 34, (lane >= 34) & (lane < 36))
        )
    m = iota((1, LANES), 1)
    left = block(3, m >> 1, 30 + (m & 1), m < 64)
    right = block(4, m >> 1, m & 1, m < 64)
    lanes = iota((CH, LANES), 1)

    def put(r, row):
        pad_ref[r] = row.astype(BF16)
        for b in range(5):
            pb[b, r] = roll(row, -b) if b else row

    for k in range(2):
        put(k, rows[0][:, LANES * k : LANES * (k + 1)])
        put(34 + k, rows[1][:, LANES * k : LANES * (k + 1)])
    for g in range(GROUPS):
        chunk = x_ref[:, LANES * g : LANES * (g + 1)].astype(F32)
        for k in range(4):
            r = 4 * g + k
            row = roll(chunk, 2 - 32 * k)
            row = jnp.where(lanes < 2, roll(left, -2 * r), row)
            put(r + 2, jnp.where(lanes >= 34, roll(right, 34 - 2 * r), row))

    def group(g, carry):
        out = jnp.zeros((CH, LANES), F32)
        for k in range(4):
            acc = jnp.zeros((CH, LANES), F32)
            for a in range(5):
                for b in range(5):
                    acc = acc + kb[5 * a + b] * pb[b, 4 * g + k + a]
            out = jnp.where(lanes >> 5 == k, roll(acc, 32 * k), out)
        hid_ref[g] = out.astype(BF16)
        return carry

    lax.fori_loop(0, GROUPS, group, 0)


def dense_kernel(feat_ref, cot_ref, win_ref, wout_ref, br_ref, gf_ref, g_ref):
    feat = feat_ref[...].reshape(FULL, LANES)
    cot = cot_ref[...].reshape(FULL, LANES)
    branch = jnp.zeros((FULL, LANES), F32)
    gfeat = jnp.zeros((FULL, LANES), F32)
    for part in range(4):
        lo = FULL * part
        w_in = win_ref[:, lo : lo + FULL]
        w_out = wout_ref[lo : lo + FULL, :]
        pre = dot(w_in, feat, ((0,), (0,)))
        cumul = 0.5 * (1.0 + lax.erf(pre * 0.7071067811865476))
        act = (pre * cumul).astype(BF16)
        gact = dot(w_out, cot)
        slope = cumul + pre * jnp.exp(-0.5 * pre * pre) * 0.3989422804014327
        gpre = (gact * slope).astype(BF16)
        branch = branch + dot(w_out, act, ((0,), (0,)))
        gfeat = gfeat + dot(w_in, gpre)
        g_ref[lo : lo + FULL, :] = dot(act, cot, ((1,), (1,)))
        g_ref[HID + lo : HID + lo + FULL, :] = dot(feat, gpre, ((1,), (1,)))
    br_ref[...] = branch.astype(BF16).reshape(GROUPS, CH, LANES)
    gf_ref[...] = gfeat.astype(BF16).reshape(GROUPS, CH, LANES)


def back_kernel(x_ref, bo_ref, gh_ref, go_ref, k_ref, pad_ref, out_ref, acc_ref, bt_ref, kg_ref, pb, gb, gp, kb, ka):
    spread_taps(k_ref, kb)
    lanes = iota((CH, LANES), 1)
    zero = jnp.zeros((CH, LANES), F32)
    for r in range(4):
        for b in range(5):
            gb[b, r] = zero
            gb[b, SIDE + 4 + r] = zero
    for g in range(GROUPS):
        span = slice(LANES * g, LANES * (g + 1))
        out_ref[:, span] = (x_ref[:, span].astype(F32) + bo_ref[g].astype(F32)).astype(BF16)
        chunk = gh_ref[g].astype(F32)
        for k in range(4):
            row = jnp.where(lanes < 32, roll(chunk, -32 * k) if k else chunk, 0.0)
            for b in range(5):
                gb[b, 4 * g + k + 4] = roll(row, b) if b else row

    def shift(r, carry):
        row = pad_ref[r].astype(F32)
        for b in range(5):
            pb[b, r] = roll(row, -b) if b else row
        return carry

    lax.fori_loop(0, PADS, shift, 0)

    def spread(q, carry):
        acc = zero
        for a in range(5):
            for b in range(5):
                acc = acc + kb[5 * a + b] * gb[b, q + (4 - a)]
        gp[q] = acc
        return carry

    lax.fori_loop(0, PADS, spread, 0)
    for b in range(5):

        def taps(u, sums, b=b):
            grad = gb[0, u + 4]
            return tuple(sums[a] + grad * pb[b, u + a] for a in range(5))

        sums = lax.fori_loop(0, SIDE, taps, (zero,) * 5)
        for a in range(5):
            ka[5 * a + b] = sums[a]
    for tap in range(TAPS, 28):
        ka[tap] = zero
    totals = dot(jnp.ones((8, LANES), F32), ka[...].reshape(28 * CH, LANES), ((1,), (1,)), lax.Precision.HIGHEST)
    sub = iota((8, LANES), 0)
    kg = jnp.zeros((8, LANES), F32)
    for i in range(7):
        kg = jnp.where(sub == i, totals[:, LANES * i : LANES * (i + 1)], kg)
    kg_ref[...] = kg

    top, left, right, bottom, corners = zero, zero, zero, zero, zero
    for line in range(2):
        upper, lower = gp[line], gp[34 + line]
        top = jnp.where(lanes >> 5 == line, roll(upper, 32 * line - 2), top)
        bottom = jnp.where(lanes >> 5 == line, roll(lower, 32 * line - 2), bottom)
        for i, (row, first) in enumerate(((upper, 0), (upper, 34), (lower, 0), (lower, 34))):
            corners = jnp.where(lanes >> 1 == 2 * i + line, roll(row, 4 * i + 2 * line - first), corners)
    for g in range(GROUPS):
        span = slice(LANES * g, LANES * (g + 1))
        total = zero
        for k in range(4):
            r = 4 * g + k
            row = gp[r + 2]
            left = jnp.where(lanes >> 1 == r, roll(row, 2 * r), left)
            right = jnp.where(lanes >> 1 == r, roll(row, 2 * r - 34), right)
            total = jnp.where(lanes >> 5 == k, roll(row, 32 * k - 2), total)
        acc_ref[g] = total + go_ref[:, span].astype(F32)
    for i, wide in enumerate((top, left, right, bottom, corners)):
        bt_ref[i] = fold(wide).astype(BF16)


def last_kernel(nb_ref, rot_ref, acc_ref, sel_ref, o_ref):
    me = lax.axis_index("tile")
    k = iota((LANES, 1), 0)
    p = iota((1, 1024), 1)
    total = jnp.zeros((CH, 1024), F32)
    for index, d in enumerate(EDGE_DIRS):
        q = rot_ref[nb_ref[me, 7 - d], d]
        line, along = ((k >> 5), (k & 31)) if d in (1, 6) else ((k & 1), (k >> 1))
        edge = line + (30 if d in (1, 3) else 0)
        si, sj = turned(q, edge, along) if d in (1, 6) else turned(q, along, edge)
        place = jnp.where((p == si * 32 + sj) & (k < 64), 1.0, 0.0).astype(BF16)
        total = total + dot(unfold(sel_ref[index]), place)
    q = jnp.zeros((LANES, 1), I32)
    for index, d in enumerate(CORNER_DIRS):
        q = jnp.where(k >> 2 == index, rot_ref[nb_ref[me, 7 - d], d], q)
    i = ((k >> 1) & 1) + jnp.where(k < 8, 30, 0)
    j = (k & 1) + jnp.where((k >> 2) & 1 == 0, 30, 0)
    si, sj = turned(q, i, j)
    place = jnp.where((p == si * 32 + sj) & (k < 16), 1.0, 0.0).astype(BF16)
    total = total + dot(unfold(sel_ref[4]), place)
    for g in range(GROUPS):
        span = slice(LANES * g, LANES * (g + 1))
        o_ref[:, span] = (acc_ref[g] + total[:, span]).astype(BF16)


class Place:
    def __init__(self):
        self.tile, self.chan = lax.axis_index("tile"), lax.axis_index("chan")
        self.z = lax.rem(self.tile, NZ)
        self.xy = lax.div(self.tile, NZ)
        self.x = lax.rem(self.xy, NX)
        self.yl = lax.div(self.xy, NX)
        self.core = lax.rem(self.chan, 2)
        self.yh = lax.div(self.chan, 2)
        self.y = self.yh * NYL + self.yl

    def at(self, tile, chan):
        return {"tile": tile, "chan": chan}

    def along_z(self, k):
        return self.at(self.xy * NZ + lax.rem(self.z + k, NZ), self.chan)

    def tile_xy(self, k):
        return lax.rem(self.xy + k, NXY) * NZ + self.z

    def along_xy(self, k):
        return self.at(self.tile_xy(k), self.chan)

    def along_x(self, k):
        return self.at((self.yl * NX + lax.rem(self.x + k, NX)) * NZ + self.z, self.chan)

    def along_yl(self, k):
        return self.at((lax.rem(self.yl + k, NYL) * NX + self.x) * NZ + self.z, self.chan)

    def along_y(self, k):
        y = lax.rem(self.y + k, NY)
        return self.at((lax.rem(y, NYL) * NX + self.x) * NZ + self.z, lax.div(y, NYL) * 2 + self.core)

    def along_chan(self, k):
        return self.at(self.tile, lax.rem(self.chan + k, NCHAN))

    def partner(self):
        return self.at(self.tile, self.yh * 2 + (1 - self.core))


def meet(devices):
    barrier = pltpu.get_barrier_semaphore()
    for device in devices:
        pl.semaphore_signal(barrier, inc=1, device_id=device, device_id_type=MESH)
    pl.semaphore_wait(barrier, len(devices))


def send(src, dst, sems, k, device):
    copy = pltpu.make_async_remote_copy(
        src_ref=src, dst_ref=dst, send_sem=sems[0].at[k], recv_sem=sems[1].at[k], device_id=device, device_id_type=MESH
    )
    copy.start()
    return copy


def landed(copies):
    for copy in copies:
        copy.wait_recv()


def sent(copies):
    for copy in copies:
        copy.wait_send()


def gather_kernel(nb_ref, rot_ref, rim_ref, go_ref, sel_ref, cot_ref, zbuf, out, got, *sems):
    at = Place()
    z_sems, xy_sems, chan_sems = sems[0:2], sems[2:4], sems[4:6]
    meet(
        [at.along_z(k) for k in range(1, NZ)]
        + [at.along_xy(k) for k in range(1, NXY)]
        + [at.along_chan(k) for k in range(1, NCHAN)]
    )
    along_z = [send(rim_ref, zbuf.at[k], z_sems, k, at.along_z(k)) for k in range(1, NZ)]
    zbuf[0] = rim_ref[...]
    along_chan = []
    for k in range(1, NCHAN):
        chan = lax.rem(at.chan + k, NCHAN)
        chunk = go_ref.at[:, pl.ds(pl.multiple_of(chan * LANES, LANES), LANES)]
        along_chan.append(send(chunk, cot_ref.at[at.chan], chan_sems, k, at.along_chan(k)))
    cot_ref[at.chan] = go_ref[:, pl.ds(pl.multiple_of(at.chan * LANES, LANES), LANES)]
    landed(along_z)
    along_xy = []
    for k in range(NXY):
        tile = at.tile_xy(k)
        for d in range(8):
            source = nb_ref[tile, d]
            slot = lax.rem(at.z - lax.rem(source, NZ) + NZ, NZ)
            edge = (rot_ref[tile, d] + BASE[d]) & 3
            out[k, d] = zbuf[slot, edge]
        if k:
            along_xy.append(send(out.at[k], got.at[k], xy_sems, k, at.along_xy(k)))
    got[0] = out[0]
    landed(along_xy)
    for d in range(8):
        slot = lax.rem(at.xy - lax.div(nb_ref[at.tile, d], NZ) + NXY, NXY)
        sel_ref[d] = got[slot, d]
    landed(along_chan)
    sent(along_z + along_chan + along_xy)


def swap_kernel(count, *refs):
    srcs, dsts, sems = refs[:count], refs[count : 2 * count], refs[2 * count :]
    at = Place()
    meet([at.along_chan(k) for k in range(1, NCHAN)])
    copies = []
    for index in range(count):
        for k in range(1, NCHAN):
            chan = lax.rem(at.chan + k, NCHAN)
            pair = sems[2 * index : 2 * index + 2]
            copies.append(send(srcs[index].at[chan], dsts[index].at[at.chan], pair, k, at.along_chan(k)))
        dsts[index][at.chan] = srcs[index][at.chan]
    landed(copies)
    sent(copies)


def reduce_kernel(
    nb_ref, bt_ref, kg_ref, g_ref, sel_ref, win_ref, wout_ref, kgrad_ref,
    zbuf, out, got, kz, kx, ky, ksum, kall, ra, sa, rb, sb, rc, sc, rd, ey, fx, hc, *sems
):
    at = Place()
    pairs = [sems[2 * i : 2 * i + 2] for i in range(len(sems) // 2)]
    s_hz, s_hxy, s_kz, s_kx, s_ky, s_kc, s_core, s_x, s_y, s_z, s_ay, s_ax, s_ac = pairs
    meet(
        [at.along_z(k) for k in range(1, NZ)]
        + [at.along_xy(k) for k in range(1, NXY)]
        + [at.along_chan(k) for k in range(1, NCHAN)]
        + [at.along_y(k) for k in range(1, NY)]
    )
    copies = []

    def go(*args):
        copies.append(send(*args))
        return copies[-1]

    half = HID
    other = pl.ds(pl.multiple_of((1 - at.core) * half, half), half)
    mine = pl.ds(pl.multiple_of(at.core * half, half), half)
    core = [go(g_ref.at[other], ra, s_core, 0, at.partner())]
    halo_z = [go(bt_ref, zbuf.at[k], s_hz, k, at.along_z(k)) for k in range(1, NZ)]
    grad_z = [go(kg_ref, kz.at[k], s_kz, k, at.along_z(k)) for k in range(1, NZ)]
    zbuf[0] = bt_ref[...]
    landed(core)
    sa[...] = g_ref[mine] + ra[...]
    part_x = half // NX
    sum_x = []
    for k in range(1, NX):
        rows = pl.ds(pl.multiple_of(lax.rem(at.x + k, NX) * part_x, part_x), part_x)
        sum_x.append(go(sa.at[rows], rb.at[k], s_x, k, at.along_x(k)))

    landed(halo_z)
    lane = iota((16, LANES), 1)
    halo_xy = []
    for k in range(NXY):
        tile = at.tile_xy(k)
        packed = jnp.zeros((16, LANES), BF16)
        for i in range(4):
            slot = lax.rem(at.z - lax.rem(nb_ref[tile, 7 - EDGE_DIRS[i]], NZ) + NZ, NZ)
            out[k, i] = zbuf[slot, i]
            slot = lax.rem(at.z - lax.rem(nb_ref[tile, 7 - CORNER_DIRS[i]], NZ) + NZ, NZ)
            packed = jnp.where((lane >> 2) & 15 == i, zbuf[slot, 4], packed)
        out[k, 4] = packed
        if k:
            halo_xy.append(go(out.at[k], got.at[k], s_hxy, k, at.along_xy(k)))
    got[0] = out[0]

    landed(grad_z)
    total = kg_ref[...]
    for k in range(1, NZ):
        total = total + kz[k]
    ksum[0] = total
    grad_x = [go(ksum.at[0], kx.at[k], s_kx, k, at.along_x(k)) for k in range(1, NX)]

    landed(sum_x)
    total = sa[pl.ds(pl.multiple_of(at.x * part_x, part_x), part_x)]
    for k in range(1, NX):
        total = total + rb[k]
    sb[...] = total
    part_y = part_x // NY
    sum_y = []
    for k in range(1, NY):
        rows = pl.ds(pl.multiple_of(lax.rem(at.y + k, NY) * part_y, part_y), part_y)
        sum_y.append(go(sb.at[rows], rc.at[k], s_y, k, at.along_y(k)))

    landed(grad_x)
    total = ksum[0]
    for k in range(1, NX):
        total = total + kx[k]
    ksum[1] = total
    grad_y = [go(ksum.at[1], ky.at[k], s_ky, k, at.along_yl(k)) for k in range(1, NYL)]

    landed(halo_xy)
    packed = jnp.zeros((16, LANES), BF16)
    for i in range(4):
        slot = lax.rem(at.xy - lax.div(nb_ref[at.tile, 7 - EDGE_DIRS[i]], NZ) + NXY, NXY)
        sel_ref[i] = got[slot, i]
        slot = lax.rem(at.xy - lax.div(nb_ref[at.tile, 7 - CORNER_DIRS[i]], NZ) + NXY, NXY)
        packed = jnp.where((lane >> 2) & 15 == i, got[slot, 4], packed)
    sel_ref[4] = packed

    landed(sum_y)
    total = sb[pl.ds(pl.multiple_of(at.y * part_y, part_y), part_y)]
    for k in range(1, NY):
        total = total + rc[k]
    sc[...] = total
    sum_z = [go(sc, rd.at[k], s_z, k, at.along_z(k)) for k in range(1, NZ)]

    landed(grad_y)
    ksum[2] = (ksum[1] + ky[1]) * SCALE
    kall[at.chan] = ksum[2]
    grad_c = [go(ksum.at[2], kall.at[at.chan], s_kc, k, at.along_chan(k)) for k in range(1, NCHAN)]

    landed(sum_z)
    total = sc[...]
    for k in range(1, NZ):
        total = total + rd[k]
    ey[at.y] = (total * SCALE).astype(BF16)
    all_y = [go(ey.at[at.y], ey.at[at.y], s_ay, k, at.along_y(k)) for k in range(1, NY)]

    landed(grad_c)
    low = iota((8, LANES), 1) >> 5
    for j in range(4):
        for side in range(2):
            rows = jnp.zeros((8, LANES), F32)
            for k in range(4):
                rows = jnp.where(low == k, roll(kall[4 * side + k], 32 * (k - j)), rows)
            for i in range(7):
                if 4 * i + j < TAPS:
                    kgrad_ref[4 * i + j : 4 * i + j + 1, LANES * side : LANES * (side + 1)] = rows[i : i + 1]

    landed(all_y)
    for y in range(NY):
        fx[at.x, part_y * y : part_y * (y + 1)] = ey[y]
    all_x = [go(fx.at[at.x], fx.at[at.x], s_ax, k, at.along_x(k)) for k in range(1, NX)]
    landed(all_x)
    all_c = [go(fx, hc, s_ac, 0, at.partner())]

    def place(refs, first):
        for x in range(NX):
            values = refs[x].astype(F32)
            if first:
                wout_ref[part_x * x : part_x * (x + 1), :] = values
            else:
                win_ref[:, part_x * x : part_x * (x + 1)] = values

    @pl.when(at.core == 0)
    def _():
        place(fx, True)

    @pl.when(at.core == 1)
    def _():
        place(fx, False)

    landed(all_c)

    @pl.when(at.core == 0)
    def _():
        place(hc, False)

    @pl.when(at.core == 1)
    def _():
        place(hc, True)

    sent(copies)


def dma(count):
    return [pltpu.SemaphoreType.DMA((count,))] * 2


def call(kernel, outs, ins, scratch=(), smem=0, remote=None, name=None):
    params = {} if remote is None else dict(collective_id=remote, has_side_effects=True)
    return pl.pallas_call(
        kernel,
        out_shape=[jax.ShapeDtypeStruct(shape, dtype) for shape, dtype in outs],
        in_specs=[SMEM] * smem + [VMEM] * (len(ins) - smem),
        out_specs=[VMEM] * len(outs),
        scratch_shapes=list(scratch),
        compiler_params=pltpu.CompilerParams(vmem_limit_bytes=48 << 20, **params),
        name=name,
    )(*ins)


def body(inputs, grad_out, kernel, w_in, w_out, neighbours, rotations):
    x = inputs.reshape(CH, 1024)
    go = grad_out.reshape(CH, 1024)
    chunks = (GROUPS, CH, LANES)
    (rims,) = call(rim_kernel, [((4, 16, LANES), BF16)], [x], name="rims")
    sel, cot = call(
        gather_kernel,
        [((8, 16, LANES), BF16), (chunks, BF16)],
        [neighbours, rotations, rims, go],
        [
            pltpu.VMEM((NZ, 4, 16, LANES), BF16),
            pltpu.VMEM((NXY, 8, 16, LANES), BF16),
            pltpu.VMEM((NXY, 8, 16, LANES), BF16),
            *dma(NZ), *dma(NXY), *dma(NCHAN),
        ],
        smem=2, remote=1, name="halo",
    )
    hid, padded = call(
        conv_kernel,
        [(chunks, BF16), ((PADS, CH, LANES), BF16)],
        [rotations, x, sel, kernel],
        [pltpu.VMEM((5, PADS, CH, LANES), F32), pltpu.VMEM((TAPS, CH, LANES), F32)],
        smem=1, name="conv",
    )
    (feat,) = call(lambda *refs: swap_kernel(1, *refs), [(chunks, BF16)], [hid], dma(NCHAN), remote=2, name="swap1")
    branch, gfeat, grads = call(
        dense_kernel,
        [(chunks, BF16), (chunks, BF16), ((2 * HID, FULL), F32)],
        [feat, cot, w_in, w_out],
        name="dense",
    )
    bo, gh = call(
        lambda *refs: swap_kernel(2, *refs), [(chunks, BF16)] * 2, [branch, gfeat], dma(NCHAN) * 2, remote=3, name="swap2"
    )
    outputs, acc, border, kg = call(
        back_kernel,
        [((CH, 1024), BF16), (chunks, F32), ((5, 16, LANES), BF16), ((8, LANES), F32)],
        [x, bo, gh, go, kernel, padded],
        [
            pltpu.VMEM((5, PADS, CH, LANES), F32),
            pltpu.VMEM((5, SIDE + 8, CH, LANES), F32),
            pltpu.VMEM((PADS, CH, LANES), F32),
            pltpu.VMEM((TAPS, CH, LANES), F32),
            pltpu.VMEM((28, CH, LANES), F32),
        ],
        name="back",
    )
    part_x = HID // NX
    part_y = part_x // NY
    sel2, grad_w_in, grad_w_out, grad_kernel = call(
        reduce_kernel,
        [((5, 16, LANES), BF16), ((FULL, HID), F32), ((HID, FULL), F32), ((TAPS, FULL), F32)],
        [neighbours, border, kg, grads],
        [
            pltpu.VMEM((NZ, 5, 16, LANES), BF16),
            pltpu.VMEM((NXY, 5, 16, LANES), BF16),
            pltpu.VMEM((NXY, 5, 16, LANES), BF16),
            pltpu.VMEM((NZ, 8, LANES), F32),
            pltpu.VMEM((NX, 8, LANES), F32),
            pltpu.VMEM((NYL, 8, LANES), F32),
            pltpu.VMEM((3, 8, LANES), F32),
            pltpu.VMEM((NCHAN, 8, LANES), F32),
            pltpu.VMEM((HID, FULL), F32),
            pltpu.VMEM((HID, FULL), F32),
            pltpu.VMEM((NX, part_x, FULL), F32),
            pltpu.VMEM((part_x, FULL), F32),
            pltpu.VMEM((NY, part_y, FULL), F32),
            pltpu.VMEM((part_y, FULL), F32),
            pltpu.VMEM((NZ, part_y, FULL), F32),
            pltpu.VMEM((NY, part_y, FULL), BF16),
            pltpu.VMEM((NX, part_x, FULL), BF16),
            pltpu.VMEM((NX, part_x, FULL), BF16),
            *dma(NZ), *dma(NXY), *dma(NZ), *dma(NX), *dma(NYL), *dma(NCHAN),
            *dma(1), *dma(NX), *dma(NY), *dma(NZ), *dma(NY), *dma(NX), *dma(1),
        ],
        smem=1, remote=4, name="reduce",
    )
    (grad_in,) = call(last_kernel, [((CH, 1024), BF16)], [neighbours, rotations, acc, sel2], smem=2, name="last")
    return outputs.reshape(1, CH, 1024), grad_in.reshape(1, CH, 1024), grad_w_in, grad_w_out, grad_kernel


def solution(mesh):
    split = P("tile", "chan", None)
    return jax.shard_map(
        body,
        mesh=mesh,
        in_specs=(split, split, P(None, "chan"), P(), P(), P(), P()),
        out_specs=(split, split, P(), P(), P()),
        check_vma=False,
    )
```

time: 1610 us -> 153 us (0.10)
  the two profiles are of different devices: /device:TPU:16 before, /device:TPU:1 now
where the time goes in v1:
time: 153 us; the launch traced here: 152 us
  Pallas kernels  140 us (92%)
  local copies, waits for them, and re-layouts  11.8 us (8%)
    pallas_call x9, Pallas kernels, call(): pl.pallas_call(kernel, out_shape=[jax.ShapeDtypeStruct(shape, dtype) for...  140 us
    unnamed x23, local copies, waits for them, and re-layouts  11.8 us

profile of v1, /device:TPU:1, one launch (start us, length us, event | category | flops | bytes accessed | tf_op | source)
XLA Modules:
  0.0 152.3 jit_solution(5514875048445773454)
XLA Ops:
  0.6 0.0 copy-start
  0.6 0.8 copy-done
  1.5 0.3 rims.1.rim_ref
  1.8 0.8 copy.12.nb_ref
  2.5 0.8 copy.14.rot_ref
  3.3 0.0 copy-start.5
  3.3 0.8 copy-done.5
  4.2 36.6 %halo.1 = (bf16[8,16,128]{2,1,0:T(8,128)(2,1)S(1)}, bf16[8,32,128]{2,1,0:T(8,128)(2,1)S(1)}) custom-call(s32[96,8]{1,0:T(8,128)S(1)} %copy.12.nb_ref, s32[96,8]{1,0:T(8,128)S(1)} %copy.14.rot_ref, bf16[4,16,128]{2,1,0:T(8,128)(2,1)S(1)} %rims.1.rim_ref, bf16[32,1024]{1,0:T(8,128)(2,1)S(1)} %bitcast.7), custom_call_target="tpu_custom_call" | custom-call | tf_op jit(solution)/shard_map/halo/pallas_call | solution.py:539
  40.8 0.0 copy-start.1
  40.8 0.8 copy-done.1
  41.6 0.0 copy-start.7
  41.6 0.7 copy-done.7
  42.3 5.5 %conv.1 = (bf16[8,32,128]{2,1,0:T(8,128)(2,1)S(1)}, bf16[36,32,128]{2,1,0:T(8,128)(2,1)S(1)}) custom-call(s32[96,8]{1,0:T(8,128)S(1)} %copy.14.rot_ref, bf16[32,1024]{1,0:T(8,128)(2,1)S(1)} %bitcast.5, bf16[8,16,128]{2,1,0:T(8,128)(2,1)S(1)} %get-tuple-element.22.sel_ref, bf16[25,32]{1,0:T(8,128)(2,1)S(1)} %copy-done.7), custom_call_target="tpu_custom_call" | custom-call | tf_op jit(solution)/shard_map/conv/pallas_call | solution.py:539
  47.8 9.1 %swap1.1.feat_ref = bf16[8,32,128]{2,1,0:T(8,128)(2,1)S(1)} custom-call(bf16[8,32,128]{2,1,0:T(8,128)(2,1)S(1)} %get-tuple-element.23.refs_0_), custom_call_target="tpu_custom_call" | custom-call | tf_op jit(solution)/shard_map/swap1/pallas_call | solution.py:539
  56.9 0.0 copy-start.3
  56.9 1.0 copy-done.3
  58.0 0.0 copy-start.4
  58.0 1.0 copy-done.4
  59.0 1.5 dense.1
  60.5 10.3 %swap2.1 = (bf16[8,32,128]{2,1,0:T(8,128)(2,1)S(1)}, bf16[8,32,128]{2,1,0:T(8,128)(2,1)S(1)}) custom-call(bf16[8,32,128]{2,1,0:T(8,128)(2,1)S(1)} %get-tuple-element.25.refs_0_, bf16[8,32,128]{2,1,0:T(8,128)(2,1)S(1)} %get-tuple-element.26.refs_1_), custom_call_target="tpu_custom_call" | custom-call | tf_op jit(solution)/shard_map/swap2/pallas_call | solution.py:539
  70.8 0.0 copy-start.2
  70.8 0.8 copy-done.2
  71.6 0.0 copy-start.6
  71.6 0.8 copy-done.6
  72.5 0.0 copy-start.8
  72.5 0.7 copy-done.8
  73.2 9.1 %back.1 = (bf16[32,1024]{1,0:T(8,128)(2,1)}, f32[8,32,128]{2,1,0:T(8,128)S(1)}, bf16[5,16,128]{2,1,0:T(8,128)(2,1)S(1)}, f32[8,128]{1,0:T(8,128)S(1)}) custom-call(bf16[32,1024]{1,0:T(8,128)(2,1)S(1)} %bitcast.6, bf16[8,32,128]{2,1,0:T(8,128)(2,1)S(1)} %get-tuple-element.27.bo_ref, bf16[8,32,128]{2,1,0:T(8,128)(2,1)S(1)} %get-tuple-element.28.gh_ref, ...), custom_call_target="tpu_custom_call" | custom-call | tf_op jit(solution)/shard_map/back/pallas_call | solution.py:539
  82.3 64.3 %reduce.1 = (bf16[5,16,128]{2,1,0:T(8,128)(2,1)S(1)}, f32[256,1024]{1,0:T(8,128)S(1)}, f32[1024,256]{1,0:T(8,128)S(1)}, f32[25,256]{1,0:T(8,128)S(1)}) custom-call(s32[96,8]{1,0:T(8,128)S(1)} %copy.12.nb_ref, bf16[5,16,128]{2,1,0:T(8,128)(2,1)S(1)} %get-tuple-element.32.bt_ref, f32[8,128]{1,0:T(8,128)S(1)} %get-tuple-element.33.kg_ref, ...), custom_call_target="tpu_custom_call" | custom-call | tf_op jit(solution)/shard_map/reduce/pallas_call | solution.py:539
  146.6 3.2 %last.1 = bf16[32,1024]{1,0:T(8,128)(2,1)} custom-call(s32[96,8]{1,0:T(8,128)S(1)} %copy.12.nb_ref, s32[96,8]{1,0:T(8,128)S(1)} %copy.14.rot_ref, f32[8,32,128]{2,1,0:T(8,128)S(1)} %get-tuple-element.31.acc_ref, bf16[5,16,128]{2,1,0:T(8,128)(2,1)S(1)} %get-tuple-element.35.sel_ref), custom_call_target="tpu_custom_call" | custom-call | tf_op jit(solution)/shard_map/last/pallas_call | solution.py:539
  149.7 1.0 copy.21
  150.7 1.0 copy.22
  151.7 0.6 copy.23
Async XLA Ops:
  0.6 0.8 copy-start
  3.3 0.8 copy-start.5
  40.8 0.8 copy-start.1
  41.6 0.7 copy-start.7
  56.9 1.0 copy-start.3
  58.0 1.0 copy-start.4
  70.8 0.8 copy-start.2
  71.6 0.8 copy-start.6
  72.5 0.7 copy-start.8

commit v2 on v1

v2 whole, which is shorter than its diff:
```python
import jax
import jax.numpy as jnp
from jax import lax
from jax.experimental import pallas as pl
from jax.experimental.pallas import tpu as pltpu
from jax.sharding import PartitionSpec as P

NX, NZ, NYL, NYH = 4, 12, 2, 4
NXY = NX * NYL
NY = NYL * NYH
NCHAN = NYH * 2
CH = 32
SIDE = 32
LANES = 128
GROUPS = 8
PADS = SIDE + 4
TAPS = 25
HID = 1024
FULL = 256
SCALE = (NXY * NZ * SIDE * SIDE) ** -0.5
MESH = pl.DeviceIdType.MESH
F32, BF16, I32 = jnp.float32, jnp.bfloat16, jnp.int32

BASE = (0, 0, 0, 3, 1, 2, 2, 2)
EDGE_DIRS = (1, 3, 4, 6)
CORNER_DIRS = (0, 2, 5, 7)

VMEM = pl.BlockSpec(memory_space=pltpu.VMEM)
SMEM = pl.BlockSpec(memory_space=pltpu.SMEM)


def iota(shape, axis):
    return lax.broadcasted_iota(I32, shape, axis)


def roll(values, shift):
    return pltpu.roll(values, shift % LANES, 1)


def dot(a, b, contract=((1,), (0,)), precision=None):
    return lax.dot_general(a, b, (contract, ((), ())), preferred_element_type=F32, precision=precision)


def turned(q, i, j):
    q0, q1, q2, q3 = [(q == k).astype(I32) for k in range(4)]
    rows = q0 * i + q1 * j + q2 * (31 - i) + q3 * (31 - j)
    cols = q0 * j + q1 * (31 - i) + q2 * (31 - j) + q3 * i
    return rows, cols


def fold(wide):
    low = iota((16, LANES), 1) < 64
    return jnp.where(low, wide[:16], roll(wide[16:], 64))


def unfold(tile):
    tile = tile.astype(F32)
    return jnp.concatenate([tile, roll(tile, 64)], axis=0).astype(BF16)


def spread_taps(k_ref, kb):
    taps = k_ref[...].astype(F32)
    eye = iota((CH, CH), 0) == iota((CH, CH), 1)
    ones = jnp.ones((CH, LANES), BF16)
    for tap in range(TAPS):
        row = jnp.broadcast_to(taps[tap : tap + 1, :], (CH, CH))
        kb[tap] = dot(jnp.where(eye, row, 0.0).astype(BF16), ones)


def rims_of(x_ref, rim):
    p = iota((1024, 256), 0)
    n = iota((1, 256), 1)
    e, line, i = n >> 6, (n >> 5) & 1, n & 31
    px = jnp.where(e == 0, (30 + line) * 32 + i, 0)
    px = jnp.where(e == 1, i * 32 + line, px)
    px = jnp.where(e == 2, line * 32 + i, px)
    px = jnp.where(e == 3, i * 32 + 30 + line, px)
    rims = dot(x_ref[...], jnp.where(p == px, 1.0, 0.0).astype(BF16))
    low = iota((16, LANES), 1) < 64
    for pair in range(2):
        half = rims[:, LANES * pair : LANES * (pair + 1)]
        upper, lower = half[:16], half[16:]
        rim[2 * pair] = jnp.where(low, upper, roll(lower, 64)).astype(BF16)
        rim[2 * pair + 1] = jnp.where(low, roll(upper, 64), lower).astype(BF16)


def make_picks(rot_ref, me, wide, narrow):
    def pick(d, i, j, valid):
        q = rot_ref[me, d]
        si, sj = turned(q, i, j)
        e = (q + BASE[d]) & 3
        along = (e & 1) * si + (1 - (e & 1)) * sj
        line = (1 - (e & 1)) * (si - 30 * (e == 0).astype(I32)) + (e & 1) * (sj - 30 * (e == 3).astype(I32))
        lane = jnp.where(valid, line * 32 + along, -1)
        return jnp.where(iota((LANES, lane.shape[1]), 0) == lane, 1.0, 0.0).astype(BF16)

    n = iota((1, 2 * LANES), 1)
    a, lane = n >> 7, n & 127
    for side, (first, dirs) in enumerate(((30, (0, 1, 2)), (0, (5, 6, 7)))):
        i = first + a
        wide[3 * side] = pick(dirs[0], i, 30 + lane, lane < 2)
        wide[3 * side + 1] = pick(dirs[1], i, lane - 2, (lane >= 2) & (lane < 34))
        wide[3 * side + 2] = pick(dirs[2], i, lane - 34, (lane >= 34) & (lane < 36))
    m = iota((1, LANES), 1)
    narrow[0] = pick(3, m >> 1, 30 + (m & 1), m < 64)
    narrow[1] = pick(4, m >> 1, m & 1, m < 64)


def make_places(nb_ref, rot_ref, me, places):
    k = iota((LANES, 1), 0)
    p = iota((1, 1024), 1)
    for index, d in enumerate(EDGE_DIRS):
        q = rot_ref[nb_ref[me, 7 - d], d]
        line, along = ((k >> 5), (k & 31)) if d in (1, 6) else ((k & 1), (k >> 1))
        edge = line + (30 if d in (1, 3) else 0)
        si, sj = turned(q, edge, along) if d in (1, 6) else turned(q, along, edge)
        places[index] = jnp.where((p == si * 32 + sj) & (k < 64), 1.0, 0.0).astype(BF16)
    q = jnp.zeros((LANES, 1), I32)
    for index, d in enumerate(CORNER_DIRS):
        q = jnp.where(k >> 2 == index, rot_ref[nb_ref[me, 7 - d], d], q)
    i = ((k >> 1) & 1) + jnp.where(k < 8, 30, 0)
    j = (k & 1) + jnp.where((k >> 2) & 1 == 0, 30, 0)
    si, sj = turned(q, i, j)
    places[4] = jnp.where((p == si * 32 + sj) & (k < 16), 1.0, 0.0).astype(BF16)


def inner_conv(x_ref, kb, pb, part):
    lanes = iota((CH, LANES), 1)
    zero = jnp.zeros((CH, LANES), F32)
    for r in (0, 1, 34, 35):
        for b in range(5):
            pb[b, r] = zero
    for g in range(GROUPS):
        chunk = x_ref[:, LANES * g : LANES * (g + 1)].astype(F32)
        for k in range(4):
            row = jnp.where((lanes >= 2) & (lanes < 34), roll(chunk, 2 - 32 * k), 0.0)
            for b in range(5):
                pb[b, 4 * g + k + 2] = roll(row, -b) if b else row

    def group(g, carry):
        out = zero
        for k in range(4):
            acc = zero
            for a in range(5):
                for b in range(5):
                    acc = acc + kb[5 * a + b] * pb[b, 4 * g + k + a]
            out = jnp.where(lanes >> 5 == k, roll(acc, 32 * k), out)
        part[g] = out
        return carry

    lax.fori_loop(0, GROUPS, group, 0)


def outer_conv(tiles, wide, narrow, kb, part, rows_ref, cols_ref, hid):
    lanes = iota((CH, LANES), 1)
    zero = jnp.zeros((CH, LANES), F32)
    above = dot(tiles[0], wide[0]) + dot(tiles[1], wide[1]) + dot(tiles[2], wide[2])
    below = dot(tiles[5], wide[3]) + dot(tiles[6], wide[4]) + dot(tiles[7], wide[5])
    left, right = dot(tiles[3], narrow[0]), dot(tiles[4], narrow[1])
    rows = (above[:, :LANES], above[:, LANES:], below[:, :LANES], below[:, LANES:])
    for i in range(4):
        rows_ref[i] = rows[i]
    cols_ref[0], cols_ref[1] = left, right
    first, second, last, prior = zero, zero, zero, zero
    for b in range(5):
        r0, r1, r2, r3 = [roll(row, -b) if b else row for row in rows]
        first = first + kb[b] * r0 + kb[5 + b] * r1
        second = second + kb[b] * r1
        prior = prior + kb[20 + b] * r2
        last = last + kb[15 + b] * r2 + kb[20 + b] * r3
    even = lanes & 1 == 0
    low, high = zero, zero
    for a in range(5):
        one = roll(left, -2 * (a - 2))
        low = low + kb[5 * a] * one + jnp.where(even, kb[5 * a + 1] * roll(one, -1), 0.0)
        one = roll(right, -2 * (a - 2))
        high = high + kb[5 * a + 4] * one + jnp.where(even, 0.0, kb[5 * a + 3] * roll(one, 1))
    for g in range(GROUPS):
        extra = zero
        for k in range(4):
            u = 4 * g + k
            extra = jnp.where(lanes >> 1 == 16 * k, roll(low, 32 * k - 2 * u), extra)
            extra = jnp.where(lanes >> 1 == 16 * k + 15, roll(high, 32 * k + 30 - 2 * u), extra)
        total = part[g] + extra
        if g == 0:
            total = total + jnp.where(lanes < 32, first, jnp.where(lanes < 64, roll(second, 32), 0.0))
        if g == GROUPS - 1:
            total = total + jnp.where(lanes >= 96, roll(last, 96), jnp.where(lanes >= 64, roll(prior, 64), 0.0))
        hid[g] = total.astype(BF16)


def complete_rows(rows_ref, cols_ref, pb):
    lanes = iota((CH, LANES), 1)
    left, right = cols_ref[0], cols_ref[1]
    for i, r in enumerate((0, 1, 34, 35)):
        for b in range(5):
            pb[b, r] = roll(rows_ref[i], -b) if b else rows_ref[i]
    for r in range(SIDE):
        row = jnp.where(lanes < 2, roll(left, -2 * r), pb[0, r + 2])
        row = jnp.where(lanes >> 1 == 17, roll(right, 34 - 2 * r), row)
        for b in range(5):
            pb[b, r + 2] = roll(row, -b) if b else row


def outer_spread(gh, kb, border):
    lanes = iota((CH, LANES), 1)
    zero = jnp.zeros((CH, LANES), F32)
    own = lanes < 32
    first, last = gh[0].astype(F32), gh[GROUPS - 1].astype(F32)
    r0, r1 = jnp.where(own, first, 0.0), jnp.where(own, roll(first, -32), 0.0)
    r30, r31 = jnp.where(own, roll(last, -64), 0.0), jnp.where(own, roll(last, -96), 0.0)
    gp = [zero] * 4
    for b in range(5):
        s0, s1, s30, s31 = [roll(row, b) if b else row for row in (r0, r1, r30, r31)]
        gp[0] = gp[0] + kb[b] * s0
        gp[1] = gp[1] + kb[b] * s1 + kb[5 + b] * s0
        gp[2] = gp[2] + kb[15 + b] * s31 + kb[20 + b] * s30
        gp[3] = gp[3] + kb[20 + b] * s31
    head, tail = zero, zero
    for g in range(GROUPS):
        chunk = gh[g].astype(F32)
        for k in range(4):
            r = 4 * g + k
            head = jnp.where(lanes >> 1 == r, roll(chunk, 2 * r - 32 * k), head)
            tail = jnp.where(lanes >> 1 == r, roll(chunk, 2 * r - 32 * k - 30), tail)
    even = lanes & 1 == 0
    left, right = zero, zero
    for a in range(5):
        one = roll(head, 2 * (a - 2))
        left = left + kb[5 * a] * one + jnp.where(even, 0.0, kb[5 * a + 1] * roll(one, 1))
        one = roll(tail, 2 * (a - 2))
        right = right + kb[5 * a + 4] * one + jnp.where(even, kb[5 * a + 3] * roll(one, -1), 0.0)
    top, bottom, corners = zero, zero, zero
    for line in range(2):
        upper, lower = gp[line], gp[2 + line]
        top = jnp.where(lanes >> 5 == line, roll(upper, 32 * line - 2), top)
        bottom = jnp.where(lanes >> 5 == line, roll(lower, 32 * line - 2), bottom)
        for i, (row, start) in enumerate(((upper, 0), (upper, 34), (lower, 0), (lower, 34))):
            corners = jnp.where(lanes >> 1 == 2 * i + line, roll(row, 4 * i + 2 * line - start), corners)
    for i, wide in enumerate((top, left, right, bottom, corners)):
        border[i] = fold(wide).astype(BF16)


def inner_spread(gh, go_ref, kb, gb, acc_ref):
    lanes = iota((CH, LANES), 1)
    zero = jnp.zeros((CH, LANES), F32)
    for r in (0, 1, 34, 35):
        for b in range(5):
            gb[b, r] = zero
    for g in range(GROUPS):
        chunk = gh[g].astype(F32)
        for k in range(4):
            row = jnp.where(lanes < 32, roll(chunk, -32 * k) if k else chunk, 0.0)
            for b in range(5):
                gb[b, 4 * g + k + 2] = row if b == 2 else roll(row, b - 2)
        acc_ref[g] = go_ref[:, LANES * g : LANES * (g + 1)].astype(F32)

    def group(g, carry):
        out = zero
        for k in range(4):
            acc = zero
            for a in range(5):
                for b in range(5):
                    acc = acc + kb[5 * a + b] * gb[b, 4 * g + (k + 4 - a)]
            out = jnp.where(lanes >> 5 == k, roll(acc, 32 * k), out)
        acc_ref[g] = acc_ref[g] + out
        return carry

    lax.fori_loop(0, GROUPS, group, 0)


def tap_sums(pb, gb, ka):
    zero = jnp.zeros((CH, LANES), F32)
    for b in range(5):

        def taps(u, sums, b=b):
            grad = gb[2, u + 2]
            return tuple(sums[a] + grad * pb[b, u + a] for a in range(5))

        sums = lax.fori_loop(0, SIDE, taps, (zero,) * 5)
        for a in range(5):
            ka[5 * a + b] = sums[a]
    for tap in range(TAPS, 28):
        ka[tap] = zero
    totals = dot(jnp.ones((8, LANES), F32), ka[...].reshape(28 * CH, LANES), ((1,), (1,)), lax.Precision.HIGHEST)
    sub = iota((8, LANES), 0)
    out = jnp.zeros((8, LANES), F32)
    for i in range(7):
        out = jnp.where(sub == i, totals[:, LANES * i : LANES * (i + 1)], out)
    return out


class Place:
    def __init__(self):
        self.tile, self.chan = lax.axis_index("tile"), lax.axis_index("chan")
        self.z = lax.rem(self.tile, NZ)
        self.xy = lax.div(self.tile, NZ)
        self.x = lax.rem(self.xy, NX)
        self.yl = lax.div(self.xy, NX)
        self.core = lax.rem(self.chan, 2)
        self.yh = lax.div(self.chan, 2)
        self.y = self.yh * NYL + self.yl

    def at(self, tile, chan):
        return {"tile": tile, "chan": chan}

    def along_z(self, k):
        return self.at(self.xy * NZ + lax.rem(self.z + k, NZ), self.chan)

    def tile_xy(self, k):
        return lax.rem(self.xy + k, NXY) * NZ + self.z

    def along_xy(self, k):
        return self.at(self.tile_xy(k), self.chan)

    def along_x(self, k):
        return self.at((self.yl * NX + lax.rem(self.x + k, NX)) * NZ + self.z, self.chan)

    def along_yl(self, k):
        return self.at((lax.rem(self.yl + k, NYL) * NX + self.x) * NZ + self.z, self.chan)

    def along_y(self, k):
        y = lax.rem(self.y + k, NY)
        return self.at((lax.rem(y, NYL) * NX + self.x) * NZ + self.z, lax.div(y, NYL) * 2 + self.core)

    def along_chan(self, k):
        return self.at(self.tile, lax.rem(self.chan + k, NCHAN))

    def partner(self):
        return self.at(self.tile, self.yh * 2 + (1 - self.core))


def send(src, dst, sems, k, device):
    copy = pltpu.make_async_remote_copy(
        src_ref=src, dst_ref=dst, send_sem=sems[0].at[k], recv_sem=sems[1].at[k], device_id=device, device_id_type=MESH
    )
    copy.start()
    return copy


def landed(copies):
    for copy in copies:
        copy.wait_recv()


BLOCK = 32
NEAR = (1, 7, 2, 6, 3, 5, 4)
FAR = (4, 3, 5, 2, 6, 1, 7, 0)


def scratch_shapes():
    rows, tile = (CH, LANES), (16, LANES)
    vmem = dict(
        x=((CH, 1024), BF16), go=((CH, 1024), BF16), taps=((TAPS, CH), BF16), win=((FULL, HID), BF16), wout=((HID, FULL), BF16),
        rim=((4, *tile), BF16), zbuf=((NZ, 4, *tile), BF16), xout=((NXY, 8, *tile), BF16), xgot=((NXY, 8, *tile), BF16),
        wide=((6, LANES, 2 * LANES), BF16), narrow=((2, LANES, LANES), BF16), places=((5, LANES, 1024), BF16),
        kb=((TAPS, *rows), F32), pb=((5, PADS, *rows), F32), gb=((5, PADS, *rows), F32), ka=((28, *rows), F32),
        part=((GROUPS, *rows), F32), rows=((4, *rows), F32), cols=((2, *rows), F32), acc=((GROUPS, *rows), F32),
        hid=((GROUPS, *rows), BF16), feat=((GROUPS, *rows), BF16), cot=((GROUPS, *rows), BF16),
        br=((GROUPS, *rows), BF16), gf=((GROUPS, *rows), BF16), bo=((GROUPS, *rows), BF16), gh=((GROUPS, *rows), BF16),
        border=((5, *tile), BF16), bz=((NZ, 5, *tile), BF16), bout=((NXY, 5, *tile), BF16), bgot=((NXY, 5, *tile), BF16),
        kown=((3, 8, LANES), F32), kz=((NZ, 8, LANES), F32), kxy=((NXY, 8, LANES), F32),
        grads=((2, NX, FULL, FULL), F32), terms=((2, NX, FULL, FULL), BF16), rcore=((NX, FULL, FULL), BF16),
        sx=((FULL, FULL), F32), tx=((NX, FULL, FULL), BF16), rx=((NX, NY, BLOCK, FULL), BF16),
        sy=((BLOCK, FULL), F32), ty=((NY, BLOCK, FULL), BF16), ry=((NY, BLOCK, FULL), BF16),
        tz=((BLOCK, FULL), BF16), rz=((NZ, BLOCK, FULL), BF16),
    )
    sems = dict(
        z=NZ, cot=NCHAN, xy=NXY, s1=NCHAN, s2a=NCHAN, s2b=NCHAN, core=NX, x=NX * NY, y=NY, sz=NZ, bz=NZ, bxy=NXY,
        kz=NZ, kxy=NXY, kc=NCHAN, ay=NY, ax=NX * NY, ac=NX * NY,
    )
    return vmem, sems


class Names:
    pass


def step_kernel(
    nb_hbm, rot_hbm, x_hbm, go_hbm, k_hbm, win_hbm, wout_hbm, out_ref, gin_ref, all_ref, kall_ref, load_sem, nb_ref, rot_ref, *rest
):
    vmem, semaphores = scratch_shapes()
    s, sem = Names(), Names()
    for name, ref in zip(vmem, rest):
        setattr(s, name, ref)
    rest = rest[len(vmem) :]
    for index, name in enumerate(semaphores):
        setattr(sem, name, rest[2 * index : 2 * index + 2])
    at = Place()
    copies = []

    def go(*args):
        copies.append(send(*args))
        return copies[-1]

    barrier = pltpu.get_barrier_semaphore()
    peers = (
        [at.along_z(k) for k in range(1, NZ)]
        + [at.along_xy(k) for k in range(1, NXY)]
        + [at.along_chan(k) for k in range(1, NCHAN)]
        + [at.along_y(k) for k in range(1, NY)]
    )
    for device in peers:
        pl.semaphore_signal(barrier, inc=1, device_id=device, device_id_type=MESH)
    pairs = ((x_hbm, s.x), (go_hbm, s.go), (k_hbm, s.taps), (win_hbm, s.win), (wout_hbm, s.wout), (nb_hbm, nb_ref), (rot_hbm, rot_ref))
    loads = [pltpu.make_async_copy(src, dst, load_sem.at[i]) for i, (src, dst) in enumerate(pairs)]
    for load in loads:
        load.start()
    loads[0].wait()
    rims_of(s.x, s.rim)
    loads[1].wait()
    pl.semaphore_wait(barrier, len(peers))

    z_in = [go(s.rim, s.zbuf.at[k], sem.z, k, at.along_z(k)) for k in (6, 5, 7, 4, 8, 3, 9, 2, 10, 1, 11)]
    s.zbuf[0] = s.rim[...]
    cot_in = []
    for k in range(1, NCHAN):
        chan = lax.rem(at.chan + k, NCHAN)
        chunk = s.go.at[:, pl.ds(pl.multiple_of(chan * LANES, LANES), LANES)]
        cot_in.append(go(chunk, s.cot.at[at.chan], sem.cot, k, at.along_chan(k)))
    s.cot[at.chan] = s.go[:, pl.ds(pl.multiple_of(at.chan * LANES, LANES), LANES)]
    loads[2].wait()
    spread_taps(s.taps, s.kb)
    inner_conv(s.x, s.kb, s.pb, s.part)
    loads[5].wait()
    loads[6].wait()
    make_picks(rot_ref, at.tile, s.wide, s.narrow)
    landed(z_in)
    xy_in = []
    for k in (6, 2, 5, 7, 1, 3, 4, 0):
        tile = at.tile_xy(k)
        for d in range(8):
            slot = lax.rem(at.z - lax.rem(nb_ref[tile, d], NZ) + NZ, NZ)
            s.xout[k, d] = s.zbuf[slot, (rot_ref[tile, d] + BASE[d]) & 3]
        if k:
            xy_in.append(go(s.xout.at[k], s.xgot.at[k], sem.xy, k, at.along_xy(k)))
    s.xgot[0] = s.xout[0]
    make_places(nb_ref, rot_ref, at.tile, s.places)
    loads[3].wait()
    loads[4].wait()
    landed(xy_in)
    tiles = []
    for d in range(8):
        slot = lax.rem(at.xy - lax.div(nb_ref[at.tile, d], NZ) + NXY, NXY)
        tiles.append(unfold(s.xgot[slot, d]))
    outer_conv(tiles, s.wide, s.narrow, s.kb, s.part, s.rows, s.cols, s.hid)

    def swap(src, dst, sems):
        moved = []
        for k in (4, 5, 3, 6, 2, 7, 1):
            chan = lax.rem(at.chan + k, NCHAN)
            moved.append(go(src.at[chan], dst.at[at.chan], sems, k, at.along_chan(k)))
        dst[at.chan] = src[at.chan]
        return moved

    feat_in = swap(s.hid, s.feat, sem.s1)
    complete_rows(s.rows, s.cols, s.pb)
    landed(cot_in)
    landed(feat_in)

    feat = s.feat[...].reshape(FULL, LANES)
    cot = s.cot[...].reshape(FULL, LANES)
    branch = jnp.zeros((FULL, LANES), F32)
    gfeat = jnp.zeros((FULL, LANES), F32)
    core_in = []
    for part in range(NX):
        lo = FULL * part
        w_in = s.win[:, lo : lo + FULL]
        w_out = s.wout[lo : lo + FULL, :]
        pre = dot(w_in, feat, ((0,), (0,)))
        cumul = 0.5 * (1.0 + lax.erf(pre * 0.7071067811865476))
        act = (pre * cumul).astype(BF16)
        gact = dot(w_out, cot)
        slope = cumul + pre * jnp.exp(-0.5 * pre * pre) * 0.3989422804014327
        gpre = (gact * slope).astype(BF16)
        branch = branch + dot(w_out, act, ((0,), (0,)))
        gfeat = gfeat + dot(w_in, gpre)
        for side, value in enumerate((dot(act, cot, ((1,), (1,))), dot(feat, gpre, ((1,), (1,))))):
            s.grads[side, part] = value
            s.terms[side, part] = value.astype(BF16)
    s.br[...] = branch.astype(BF16).reshape(GROUPS, CH, LANES)
    s.gf[...] = gfeat.astype(BF16).reshape(GROUPS, CH, LANES)
    grad_in = swap(s.gf, s.gh, sem.s2a)
    for part in range(NX):
        core_in.append(go(s.terms.at[1 - at.core, part], s.rcore.at[part], sem.core, part, at.partner()))
    branch_in = swap(s.br, s.bo, sem.s2b)

    landed(core_in)
    x_in = {}
    for k in (2, 1, 3, 0):
        part = lax.rem(at.x + k, NX)
        total = s.grads[at.core, part] + s.rcore[part].astype(F32)
        if k == 0:
            s.sx[...] = total
            continue
        s.tx[k] = total.astype(BF16)
        for step in FAR:
            rows = pl.ds(pl.multiple_of(lax.rem(at.y + step, NY) * BLOCK, BLOCK), BLOCK)
            x_in[k, step] = go(s.tx.at[k, rows], s.rx.at[k, step], sem.x, k * NY + step, at.along_x(k))

    landed(grad_in)
    outer_spread(s.gh, s.kb, s.border)
    border_in = [go(s.border, s.bz.at[k], sem.bz, k, at.along_z(k)) for k in (6, 5, 7, 4, 8, 3, 9, 2, 10, 1, 11)]
    s.bz[0] = s.border[...]
    inner_spread(s.gh, s.go, s.kb, s.gb, s.acc)

    y_in = {}
    for step in FAR:
        landed([x_in[k, step] for k in (1, 3, 2)])
        total = s.sx[pl.ds(pl.multiple_of(lax.rem(at.y + step, NY) * BLOCK, BLOCK), BLOCK)]
        for k in range(1, NX):
            total = total + s.rx[k, step].astype(F32)
        if step == 0:
            s.sy[...] = total
            continue
        s.ty[step] = total.astype(BF16)
        y_in[step] = go(s.ty.at[step], s.ry.at[step], sem.y, step, at.along_y(step))

    s.kown[0] = tap_sums(s.pb, s.gb, s.ka)
    taps_z = [go(s.kown.at[0], s.kz.at[k], sem.kz, k, at.along_z(k)) for k in range(1, NZ)]

    landed([y_in[step] for step in NEAR])
    total = s.sy[...]
    for step in range(1, NY):
        total = total + s.ry[step].astype(F32)
    s.sy[...] = total
    s.tz[...] = total.astype(BF16)
    sum_z = [go(s.tz, s.rz.at[k], sem.sz, k, at.along_z(k)) for k in (6, 5, 7, 4, 8, 3, 9, 2, 10, 1, 11)]

    landed(border_in)
    lane = iota((16, LANES), 1)
    border_xy = []
    for k in (6, 2, 5, 7, 1, 3, 4, 0):
        tile = at.tile_xy(k)
        packed = jnp.zeros((16, LANES), BF16)
        for i in range(4):
            slot = lax.rem(at.z - lax.rem(nb_ref[tile, 7 - EDGE_DIRS[i]], NZ) + NZ, NZ)
            s.bout[k, i] = s.bz[slot, i]
            slot = lax.rem(at.z - lax.rem(nb_ref[tile, 7 - CORNER_DIRS[i]], NZ) + NZ, NZ)
            packed = jnp.where((lane >> 2) & 15 == i, s.bz[slot, 4], packed)
        s.bout[k, 4] = packed
        if k:
            border_xy.append(go(s.bout.at[k], s.bgot.at[k], sem.bxy, k, at.along_xy(k)))
    s.bgot[0] = s.bout[0]

    landed(taps_z)
    total = s.kown[0]
    for k in range(1, NZ):
        total = total + s.kz[k]
    s.kown[1] = total
    taps_xy = [go(s.kown.at[1], s.kxy.at[k], sem.kxy, k, at.along_xy(k)) for k in range(1, NXY)]

    landed(sum_z)
    total = s.sy[...]
    for k in range(1, NZ):
        total = total + s.rz[k].astype(F32)
    all_ref[at.core, at.x, at.y] = (total * SCALE).astype(BF16)
    own = all_ref.at[at.core, at.x, at.y]
    y_all = {k: go(own, own, sem.ay, k, at.along_y(k)) for k in (4, 3, 5, 2, 6, 1, 7)}
    x_all, core_all = {}, []

    def onward(step):
        block = all_ref.at[at.core, at.x, lax.rem(at.y - step + NY, NY)]
        for k in (2, 1, 3):
            x_all[k, step] = go(block, block, sem.ax, k * NY + step, at.along_x(k))
        core_all.append(go(block, block, sem.ac, step, at.partner()))

    onward(0)

    landed(taps_xy)
    total = s.kown[1]
    for k in range(1, NXY):
        total = total + s.kxy[k]
    s.kown[2] = total * SCALE
    kall_ref[at.chan] = s.kown[2]
    taps_all = [go(s.kown.at[2], kall_ref.at[at.chan], sem.kc, k, at.along_chan(k)) for k in range(1, NCHAN)]

    for step in NEAR:
        landed([y_all[step]])
        onward(step)

    landed(branch_in)
    for g in range(GROUPS):
        span = slice(LANES * g, LANES * (g + 1))
        out_ref[:, span] = (s.x[:, span].astype(F32) + s.bo[g].astype(F32)).astype(BF16)
    landed(border_xy)
    packed = jnp.zeros((16, LANES), BF16)
    total = jnp.zeros((CH, 1024), F32)
    for i in range(4):
        slot = lax.rem(at.xy - lax.div(nb_ref[at.tile, 7 - EDGE_DIRS[i]], NZ) + NXY, NXY)
        total = total + dot(unfold(s.bgot[slot, i]), s.places[i])
        slot = lax.rem(at.xy - lax.div(nb_ref[at.tile, 7 - CORNER_DIRS[i]], NZ) + NXY, NXY)
        packed = jnp.where((lane >> 2) & 15 == i, s.bgot[slot, 4], packed)
    total = total + dot(unfold(packed), s.places[4])
    for g in range(GROUPS):
        span = slice(LANES * g, LANES * (g + 1))
        gin_ref[:, span] = (s.acc[g] + total[:, span]).astype(BF16)

    for step in (0, *NEAR):
        for k in (1, 3, 2):
            landed([x_all[k, step]])
            block = all_ref.at[at.core, lax.rem(at.x - k + NX, NX), lax.rem(at.y - step + NY, NY)]
            core_all.append(go(block, block, sem.ac, k * NY + step, at.partner()))
    landed(taps_all)
    landed(core_all)
    for copy in copies:
        copy.wait_send()


def last_kernel(out_ref, gin_ref, all_ref, kall_ref, out2_ref, gin2_ref, win_ref, wout_ref, kgrad_ref):
    out2_ref[...] = out_ref[...]
    gin2_ref[...] = gin_ref[...]
    for x in range(NX):
        for y in range(NY):
            row = FULL * x + BLOCK * y
            wout_ref[row : row + BLOCK, :] = all_ref[0, x, y].astype(F32)
            win_ref[BLOCK * y : BLOCK * (y + 1), FULL * x : FULL * (x + 1)] = all_ref[1, x, y].astype(F32)
    low = iota((8, LANES), 1) >> 5
    for j in range(4):
        for side in range(2):
            rows = jnp.zeros((8, LANES), F32)
            for k in range(4):
                rows = jnp.where(low == k, roll(kall_ref[4 * side + k], 32 * (k - j)), rows)
            for i in range(7):
                if 4 * i + j < TAPS:
                    kgrad_ref[4 * i + j : 4 * i + j + 1, LANES * side : LANES * (side + 1)] = rows[i : i + 1]


def body(inputs, grad_out, kernel, w_in, w_out, neighbours, rotations):
    vmem, semaphores = scratch_shapes()
    tables = [pltpu.SMEM((NXY * NZ, 8), I32)] * 2
    scratch = [pltpu.SemaphoreType.DMA((7,)), *tables] + [pltpu.VMEM(shape, dtype) for shape, dtype in vmem.values()]
    for count in semaphores.values():
        scratch += [pltpu.SemaphoreType.DMA((count,))] * 2
    shapes = [((CH, 1024), BF16), ((CH, 1024), BF16), ((2, NX, NY, BLOCK, FULL), BF16), ((NCHAN, 8, LANES), F32)]
    results = pl.pallas_call(
        step_kernel,
        out_shape=[jax.ShapeDtypeStruct(shape, dtype) for shape, dtype in shapes],
        in_specs=[pl.BlockSpec(memory_space=pltpu.HBM)] * 7,
        out_specs=[VMEM] * 4,
        scratch_shapes=scratch,
        compiler_params=pltpu.CompilerParams(vmem_limit_bytes=50 << 20, collective_id=1, has_side_effects=True),
        name="step",
    )(neighbours, rotations, inputs.reshape(CH, 1024), grad_out.reshape(CH, 1024), kernel, w_in, w_out)
    shapes = [((CH, 1024), BF16), ((CH, 1024), BF16), ((FULL, HID), F32), ((HID, FULL), F32), ((TAPS, FULL), F32)]
    outputs, grad_in, grad_w_in, grad_w_out, grad_kernel = pl.pallas_call(
        last_kernel,
        out_shape=[jax.ShapeDtypeStruct(shape, dtype) for shape, dtype in shapes],
        in_specs=[VMEM] * 4,
        out_specs=[VMEM] * 5,
        compiler_params=pltpu.CompilerParams(vmem_limit_bytes=12 << 20),
        name="last",
    )(*results)
    return outputs.reshape(1, CH, 1024), grad_in.reshape(1, CH, 1024), grad_w_in, grad_w_out, grad_kernel


def solution(mesh):
    split = P("tile", "chan", None)
    return jax.shard_map(
        body,
        mesh=mesh,
        in_specs=(split, split, P(None, "chan"), P(), P(), P(), P()),
        out_specs=(split, split, P(), P(), P()),
        check_vma=False,
    )
```

time: 153 us -> 89.4 us (0.58)
  Pallas kernels: 140 us -> 83.8 us
  local copies, waits for them, and re-layouts: 11.8 us -> 4.52 us
    pallas_call x9 -> x2, Pallas kernels: 140 us -> 83.8 us  [the longest x1 82.4 us: body(): pl.pallas_call(step_kernel, out_shape=[jax.ShapeDtypeStruct(shape, dtype)...]
    unnamed x23 -> x12, local copies, waits for them, and re-layouts: 11.8 us -> 4.52 us
where the time goes in v2:
time: 89.4 us; the launch traced here: 89 us
  Pallas kernels  83.8 us (94%)
  local copies, waits for them, and re-layouts  4.52 us (5%)
    pallas_call x1, Pallas kernels, body(): pl.pallas_call(step_kernel, out_shape=[jax.ShapeDtypeStruct(shape, dtype)...  82.4 us
    unnamed x12, local copies, waits for them, and re-layouts  4.52 us

profile of v2, /device:TPU:1, one launch (start us, length us, event | category | flops | bytes accessed | tf_op | source)
XLA Modules:
  0.0 89.0 jit_solution(15213444172766269435)
XLA Ops:
  0.6 0.0 copy-start.2
  0.6 0.8 copy.12.nb_hbm
  1.5 0.0 copy-start.4
  1.5 0.8 copy.13.rot_hbm
  2.2 0.0 copy-done.2
  2.2 0.0 copy-done.4
  2.3 0.0 copy-start
  2.3 1.0 %copy-done = bf16[256,1024]{1,0:T(8,128)(2,1)S(1)} copy-done((bf16[256,1024]{1,0:T(8,128)(2,1)S(1)}, bf16[256,1024]{1,0:T(8,128)(2,1)}, u32[]{:S(2)}) %copy-start) | copy-done | bytes 524312
  3.3 0.0 copy-start.1
  3.3 1.0 %copy-done.1 = bf16[1024,256]{1,0:T(8,128)(2,1)S(1)} copy-done((bf16[1024,256]{1,0:T(8,128)(2,1)S(1)}, bf16[1024,256]{1,0:T(8,128)(2,1)}, u32[]{:S(2)}) %copy-start.1) | copy-done | bytes 524312
  4.3 0.0 copy-start.3
  4.3 0.8 copy-done.3
  5.2 82.4 %step.1 = (bf16[32,1024]{1,0:T(8,128)(2,1)S(1)}, bf16[32,1024]{1,0:T(8,128)(2,1)S(1)}, bf16[2,4,8,32,256]{4,3,2,1,0:T(8,128)(2,1)S(1)}, f32[8,8,128]{2,1,0:T(8,128)S(1)}) custom-call(s32[96,8]{1,0:T(8,128)S(1)} %copy.12.nb_hbm, s32[96,8]{1,0:T(8,128)S(1)} %copy.13.rot_hbm, bf16[32,1024]{1,0:T(8,128)(2,1)S(1)} %bitcast.4, bf16[32,1024]{1,0:T(8,128)(2,1)S(1)} %bitcast.5, ...), custom_call_target="tpu_custom_call" | custom-call | tf_op jit(solution)/shard_map/step/pallas_call | solution.py:636
  87.6 1.4 %last.1 = (bf16[32,1024]{1,0:T(8,128)(2,1)}, bf16[32,1024]{1,0:T(8,128)(2,1)}, f32[256,1024]{1,0:T(8,128)}, f32[1024,256]{1,0:T(8,128)}, f32[25,256]{1,0:T(8,128)}) custom-call(bf16[32,1024]{1,0:T(8,128)(2,1)S(1)} %get-tuple-element.14.out_ref, bf16[32,1024]{1,0:T(8,128)(2,1)S(1)} %get-tuple-element.15.gin_ref, ...), custom_call_target="tpu_custom_call" | custom-call | tf_op jit(solution)/shard_map/last/pallas_call | solution.py:646
Async XLA Ops:
  0.6 1.6 %copy-start.2 = (bf16[1,32,1024]{2,1,0:T(8,128)(2,1)S(1)}, bf16[1,32,1024]{2,1,0:T(8,128)(2,1)}, u32[]{:S(2)}) copy-start(bf16[1,32,1024]{2,1,0:T(8,128)(2,1)} %param.7) | copy-start | bytes 196612
  1.5 0.8 copy-start.4
  2.3 1.0 %copy-start = (bf16[256,1024]{1,0:T(8,128)(2,1)S(1)}, bf16[256,1024]{1,0:T(8,128)(2,1)}, u32[]{:S(2)}) copy-start(bf16[256,1024]{1,0:T(8,128)(2,1)} %win_hbm.1) | copy-start | bytes 1572868
  3.3 1.0 %copy-start.1 = (bf16[1024,256]{1,0:T(8,128)(2,1)S(1)}, bf16[1024,256]{1,0:T(8,128)(2,1)}, u32[]{:S(2)}) copy-start(bf16[1024,256]{1,0:T(8,128)(2,1)} %wout_hbm.1) | copy-start | bytes 1572868
  4.3 0.8 copy-start.3

commit v3 on v2

--- a/solution.py
+++ b/solution.py
@@ -54,7 +54,6 @@
 
 
 def unfold(tile):
-    tile = tile.astype(F32)
     return jnp.concatenate([tile, roll(tile, 64)], axis=0).astype(BF16)
 
 
@@ -86,7 +85,7 @@
 
 def make_picks(rot_ref, me, wide, narrow):
     def pick(d, i, j, valid):
-        q = rot_ref[me, d]
+        q = rot_ref[d, me]
         si, sj = turned(q, i, j)
         e = (q + BASE[d]) & 3
         along = (e & 1) * si + (1 - (e & 1)) * sj
@@ -109,19 +108,23 @@
 def make_places(nb_ref, rot_ref, me, places):
     k = iota((LANES, 1), 0)
     p = iota((1, 1024), 1)
-    for index, d in enumerate(EDGE_DIRS):
-        q = rot_ref[nb_ref[me, 7 - d], d]
-        line, along = ((k >> 5), (k & 31)) if d in (1, 6) else ((k & 1), (k >> 1))
+    m = k & 63
+    pixels = []
+    for d in EDGE_DIRS:
+        q = rot_ref[d, nb_ref[7 - d, me]]
+        line, along = ((m >> 5), (m & 31)) if d in (1, 6) else ((m & 1), (m >> 1))
         edge = line + (30 if d in (1, 3) else 0)
         si, sj = turned(q, edge, along) if d in (1, 6) else turned(q, along, edge)
-        places[index] = jnp.where((p == si * 32 + sj) & (k < 64), 1.0, 0.0).astype(BF16)
+        pixels.append(si * 32 + sj)
+    for pair in range(2):
+        places[pair] = jnp.where(p == jnp.where(k < 64, pixels[2 * pair], pixels[2 * pair + 1]), 1.0, 0.0).astype(BF16)
     q = jnp.zeros((LANES, 1), I32)
     for index, d in enumerate(CORNER_DIRS):
-        q = jnp.where(k >> 2 == index, rot_ref[nb_ref[me, 7 - d], d], q)
+        q = jnp.where(k >> 2 == index, rot_ref[d, nb_ref[7 - d, me]], q)
     i = ((k >> 1) & 1) + jnp.where(k < 8, 30, 0)
     j = (k & 1) + jnp.where((k >> 2) & 1 == 0, 30, 0)
     si, sj = turned(q, i, j)
-    places[4] = jnp.where((p == si * 32 + sj) & (k < 16), 1.0, 0.0).astype(BF16)
+    places[2] = jnp.where((p == si * 32 + sj) & (k < 16), 1.0, 0.0).astype(BF16)
 
 
 def inner_conv(x_ref, kb, pb, part):
@@ -343,6 +346,13 @@
         copy.wait_recv()
 
 
+def z_slot(z, tile):
+    behind = lax.rem(z - lax.rem(tile, NZ) + NZ, NZ)
+    m = behind & 3
+    return m * 3 + lax.rem((behind >> 2) + ((m + 1) >> 2), 3)
+
+
+Z_STEPS = (0, 1, 2, 11)
 BLOCK = 32
 NEAR = (1, 7, 2, 6, 3, 5, 4)
 FAR = (4, 3, 5, 2, 6, 1, 7, 0)
@@ -352,22 +362,22 @@
     rows, tile = (CH, LANES), (16, LANES)
     vmem = dict(
         x=((CH, 1024), BF16), go=((CH, 1024), BF16), taps=((TAPS, CH), BF16), win=((FULL, HID), BF16), wout=((HID, FULL), BF16),
-        rim=((4, *tile), BF16), zbuf=((NZ, 4, *tile), BF16), xout=((NXY, 8, *tile), BF16), xgot=((NXY, 8, *tile), BF16),
-        wide=((6, LANES, 2 * LANES), BF16), narrow=((2, LANES, LANES), BF16), places=((5, LANES, 1024), BF16),
+        rim=((4, *tile), BF16), zbuf=((NZ, 4, *tile), BF16), xout=((NXY, 5, *tile), BF16), xgot=((NXY, 5, *tile), BF16),
+        wide=((6, LANES, 2 * LANES), BF16), narrow=((2, LANES, LANES), BF16), places=((3, LANES, 1024), BF16),
         kb=((TAPS, *rows), F32), pb=((5, PADS, *rows), F32), gb=((5, PADS, *rows), F32), ka=((28, *rows), F32),
         part=((GROUPS, *rows), F32), rows=((4, *rows), F32), cols=((2, *rows), F32), acc=((GROUPS, *rows), F32),
         hid=((GROUPS, *rows), BF16), feat=((GROUPS, *rows), BF16), cot=((GROUPS, *rows), BF16),
         br=((GROUPS, *rows), BF16), gf=((GROUPS, *rows), BF16), bo=((GROUPS, *rows), BF16), gh=((GROUPS, *rows), BF16),
         border=((5, *tile), BF16), bz=((NZ, 5, *tile), BF16), bout=((NXY, 5, *tile), BF16), bgot=((NXY, 5, *tile), BF16),
-        kown=((3, 8, LANES), F32), kz=((NZ, 8, LANES), F32), kxy=((NXY, 8, LANES), F32),
+        kown=((4, 8, LANES), F32), kz=((6, 8, LANES), F32), kxy=((NXY, 8, LANES), F32),
         grads=((2, NX, FULL, FULL), F32), terms=((2, NX, FULL, FULL), BF16), rcore=((NX, FULL, FULL), BF16),
         sx=((FULL, FULL), F32), tx=((NX, FULL, FULL), BF16), rx=((NX, NY, BLOCK, FULL), BF16),
         sy=((BLOCK, FULL), F32), ty=((NY, BLOCK, FULL), BF16), ry=((NY, BLOCK, FULL), BF16),
-        tz=((BLOCK, FULL), BF16), rz=((NZ, BLOCK, FULL), BF16),
+        tz=((BLOCK, FULL), BF16), uz=((BLOCK, FULL), BF16), rz=((7, BLOCK, FULL), BF16),
     )
     sems = dict(
-        z=NZ, cot=NCHAN, xy=NXY, s1=NCHAN, s2a=NCHAN, s2b=NCHAN, core=NX, x=NX * NY, y=NY, sz=NZ, bz=NZ, bxy=NXY,
-        kz=NZ, kxy=NXY, kc=NCHAN, ay=NY, ax=NX * NY, ac=NX * NY,
+        z=NZ, cot=NCHAN, xy=NXY, s1=NCHAN, s2a=NCHAN, s2b=NCHAN, core=NX, x=NX * NY, y=NY, sz=6, bz=NZ, bxy=NXY,
+        kz=6, kxy=NXY, kc=NCHAN, ay=NY, ax=NX * NY, ac=NX * NY,
     )
     return vmem, sems
 
@@ -393,9 +403,19 @@
         copies.append(send(*args))
         return copies[-1]
 
+    def first_along_z(src, slots, sems):
+        slots[0] = src[...]
+        far = [go(src, slots.at[j], sems, j, at.along_z(4 * j)) for j in (1, 2)]
+        return far, [go(src, slots.at[3 * m], sems, 3 * m, at.along_z(Z_STEPS[m])) for m in (2, 1, 3)]
+
+    def then_along_z(far, near, slots, sems):
+        for j in (1, 2):
+            landed([far[j - 1]])
+            near += [go(slots.at[j], slots.at[3 * m + j], sems, 3 * m + j, at.along_z(Z_STEPS[m])) for m in (2, 1, 3)]
+
     barrier = pltpu.get_barrier_semaphore()
     peers = (
-        [at.along_z(k) for k in range(1, NZ)]
+        [at.along_z(k) for k in (1, 2, 4, 8, 10, 11)]
         + [at.along_xy(k) for k in range(1, NXY)]
         + [at.along_chan(k) for k in range(1, NCHAN)]
         + [at.along_y(k) for k in range(1, NY)]
@@ -411,27 +431,32 @@
     loads[1].wait()
     pl.semaphore_wait(barrier, len(peers))
 
-    z_in = [go(s.rim, s.zbuf.at[k], sem.z, k, at.along_z(k)) for k in (6, 5, 7, 4, 8, 3, 9, 2, 10, 1, 11)]
-    s.zbuf[0] = s.rim[...]
+    far, z_in = first_along_z(s.rim, s.zbuf, sem.z)
     cot_in = []
     for k in range(1, NCHAN):
         chan = lax.rem(at.chan + k, NCHAN)
         chunk = s.go.at[:, pl.ds(pl.multiple_of(chan * LANES, LANES), LANES)]
         cot_in.append(go(chunk, s.cot.at[at.chan], sem.cot, k, at.along_chan(k)))
     s.cot[at.chan] = s.go[:, pl.ds(pl.multiple_of(at.chan * LANES, LANES), LANES)]
-    loads[2].wait()
+    for load in (loads[2], loads[5], loads[6]):
+        load.wait()
     spread_taps(s.taps, s.kb)
+    make_picks(rot_ref, at.tile, s.wide, s.narrow)
+    then_along_z(far, z_in, s.zbuf, sem.z)
     inner_conv(s.x, s.kb, s.pb, s.part)
-    loads[5].wait()
-    loads[6].wait()
-    make_picks(rot_ref, at.tile, s.wide, s.narrow)
     landed(z_in)
+    lane = iota((16, LANES), 1)
     xy_in = []
     for k in (6, 2, 5, 7, 1, 3, 4, 0):
         tile = at.tile_xy(k)
-        for d in range(8):
-            slot = lax.rem(at.z - lax.rem(nb_ref[tile, d], NZ) + NZ, NZ)
-            s.xout[k, d] = s.zbuf[slot, (rot_ref[tile, d] + BASE[d]) & 3]
+        packed = jnp.zeros((16, LANES), F32)
+        for i in range(4):
+            d = EDGE_DIRS[i]
+            s.xout[k, i] = s.zbuf[z_slot(at.z, nb_ref[d, tile]), (rot_ref[d, tile] + BASE[d]) & 3]
+            d = CORNER_DIRS[i]
+            edge = s.zbuf[z_slot(at.z, nb_ref[d, tile]), (rot_ref[d, tile] + BASE[d]) & 3].astype(F32)
+            packed = jnp.where(((lane + 2) & 31) >> 2 == i, roll(edge, 4 * i) if i else edge, packed)
+        s.xout[k, 4] = packed.astype(BF16)
         if k:
             xy_in.append(go(s.xout.at[k], s.xgot.at[k], sem.xy, k, at.along_xy(k)))
     s.xgot[0] = s.xout[0]
@@ -439,10 +464,15 @@
     loads[3].wait()
     loads[4].wait()
     landed(xy_in)
-    tiles = []
-    for d in range(8):
-        slot = lax.rem(at.xy - lax.div(nb_ref[at.tile, d], NZ) + NXY, NXY)
-        tiles.append(unfold(s.xgot[slot, d]))
+    tiles = [None] * 8
+    for i in range(4):
+        d = EDGE_DIRS[i]
+        slot = lax.rem(at.xy - lax.div(nb_ref[d, at.tile], NZ) + NXY, NXY)
+        tiles[d] = unfold(s.xgot[slot, i].astype(F32))
+        d = CORNER_DIRS[i]
+        slot = lax.rem(at.xy - lax.div(nb_ref[d, at.tile], NZ) + NXY, NXY)
+        packed = s.xgot[slot, 4].astype(F32)
+        tiles[d] = unfold(roll(packed, -4 * i) if i else packed)
     outer_conv(tiles, s.wide, s.narrow, s.kb, s.part, s.rows, s.cols, s.hid)
 
     def swap(src, dst, sems):
@@ -478,11 +508,10 @@
         for side, value in enumerate((dot(act, cot, ((1,), (1,))), dot(feat, gpre, ((1,), (1,))))):
             s.grads[side, part] = value
             s.terms[side, part] = value.astype(BF16)
+        core_in.append(go(s.terms.at[1 - at.core, part], s.rcore.at[part], sem.core, part, at.partner()))
     s.br[...] = branch.astype(BF16).reshape(GROUPS, CH, LANES)
     s.gf[...] = gfeat.astype(BF16).reshape(GROUPS, CH, LANES)
     grad_in = swap(s.gf, s.gh, sem.s2a)
-    for part in range(NX):
-        core_in.append(go(s.terms.at[1 - at.core, part], s.rcore.at[part], sem.core, part, at.partner()))
     branch_in = swap(s.br, s.bo, sem.s2b)
 
     landed(core_in)
@@ -500,9 +529,9 @@
 
     landed(grad_in)
     outer_spread(s.gh, s.kb, s.border)
-    border_in = [go(s.border, s.bz.at[k], sem.bz, k, at.along_z(k)) for k in (6, 5, 7, 4, 8, 3, 9, 2, 10, 1, 11)]
-    s.bz[0] = s.border[...]
+    far, border_in = first_along_z(s.border, s.bz, sem.bz)
     inner_spread(s.gh, s.go, s.kb, s.gb, s.acc)
+    then_along_z(far, border_in, s.bz, sem.bz)
 
     y_in = {}
     for step in FAR:
@@ -517,46 +546,57 @@
         y_in[step] = go(s.ty.at[step], s.ry.at[step], sem.y, step, at.along_y(step))
 
     s.kown[0] = tap_sums(s.pb, s.gb, s.ka)
-    taps_z = [go(s.kown.at[0], s.kz.at[k], sem.kz, k, at.along_z(k)) for k in range(1, NZ)]
+    taps_far = [go(s.kown.at[0], s.kz.at[j], sem.kz, j, at.along_z(4 * j)) for j in (1, 2)]
+
+    landed(branch_in)
+    for g in range(GROUPS):
+        span = slice(LANES * g, LANES * (g + 1))
+        out_ref[:, span] = (s.x[:, span].astype(F32) + s.bo[g].astype(F32)).astype(BF16)
 
     landed([y_in[step] for step in NEAR])
     total = s.sy[...]
     for step in range(1, NY):
         total = total + s.ry[step].astype(F32)
-    s.sy[...] = total
     s.tz[...] = total.astype(BF16)
-    sum_z = [go(s.tz, s.rz.at[k], sem.sz, k, at.along_z(k)) for k in (6, 5, 7, 4, 8, 3, 9, 2, 10, 1, 11)]
+    s.rz[0] = s.tz[...]
+    sum_far = [go(s.tz, s.rz.at[j], sem.sz, j, at.along_z(4 * j)) for j in (1, 2)]
+    landed(taps_far)
+    s.kown[1] = s.kown[0] + s.kz[1] + s.kz[2]
+    taps_near = [go(s.kown.at[1], s.kz.at[2 + m], sem.kz, 2 + m, at.along_z(Z_STEPS[m])) for m in (2, 1, 3)]
 
     landed(border_in)
-    lane = iota((16, LANES), 1)
     border_xy = []
     for k in (6, 2, 5, 7, 1, 3, 4, 0):
         tile = at.tile_xy(k)
         packed = jnp.zeros((16, LANES), BF16)
         for i in range(4):
-            slot = lax.rem(at.z - lax.rem(nb_ref[tile, 7 - EDGE_DIRS[i]], NZ) + NZ, NZ)
-            s.bout[k, i] = s.bz[slot, i]
-            slot = lax.rem(at.z - lax.rem(nb_ref[tile, 7 - CORNER_DIRS[i]], NZ) + NZ, NZ)
-            packed = jnp.where((lane >> 2) & 15 == i, s.bz[slot, 4], packed)
+            s.bout[k, i] = s.bz[z_slot(at.z, nb_ref[7 - EDGE_DIRS[i], tile]), i]
+            corner = s.bz[z_slot(at.z, nb_ref[7 - CORNER_DIRS[i], tile]), 4]
+            packed = jnp.where((lane >> 2) & 15 == i, corner, packed)
         s.bout[k, 4] = packed
         if k:
             border_xy.append(go(s.bout.at[k], s.bgot.at[k], sem.bxy, k, at.along_xy(k)))
     s.bgot[0] = s.bout[0]
 
-    landed(taps_z)
-    total = s.kown[0]
-    for k in range(1, NZ):
-        total = total + s.kz[k]
-    s.kown[1] = total
-    taps_xy = [go(s.kown.at[1], s.kxy.at[k], sem.kxy, k, at.along_xy(k)) for k in range(1, NXY)]
-
-    landed(sum_z)
-    total = s.sy[...]
-    for k in range(1, NZ):
-        total = total + s.rz[k].astype(F32)
+    landed(sum_far)
+    total = jnp.zeros((BLOCK, FULL), F32)
+    for third in range(3):
+        total = total + s.rz[lax.rem(lax.div(at.z, 4) - third + 3, 3)].astype(F32)
+    s.uz[...] = total.astype(BF16)
+    s.rz[3] = s.uz[...]
+    sum_near = [go(s.uz, s.rz.at[3 + m], sem.sz, 2 + m, at.along_z(Z_STEPS[m])) for m in (2, 1, 3)]
+
+    landed(taps_near)
+    s.kown[2] = s.kown[1] + s.kz[3] + s.kz[4] + s.kz[5]
+    taps_xy = [go(s.kown.at[2], s.kxy.at[k], sem.kxy, k, at.along_xy(k)) for k in range(1, NXY)]
+
+    landed(sum_near)
+    total = jnp.zeros((BLOCK, FULL), F32)
+    for quarter in range(4):
+        total = total + s.rz[3 + ((at.z - quarter + 4) & 3)].astype(F32)
     all_ref[at.core, at.x, at.y] = (total * SCALE).astype(BF16)
     own = all_ref.at[at.core, at.x, at.y]
-    y_all = {k: go(own, own, sem.ay, k, at.along_y(k)) for k in (4, 3, 5, 2, 6, 1, 7)}
+    y_all = {k: go(own, own, sem.ay, k, at.along_y(k)) for k in NEAR}
     x_all, core_all = {}, []
 
     def onward(step):
@@ -567,34 +607,37 @@
 
     onward(0)
 
-    landed(taps_xy)
-    total = s.kown[1]
-    for k in range(1, NXY):
-        total = total + s.kxy[k]
-    s.kown[2] = total * SCALE
-    kall_ref[at.chan] = s.kown[2]
-    taps_all = [go(s.kown.at[2], kall_ref.at[at.chan], sem.kc, k, at.along_chan(k)) for k in range(1, NCHAN)]
-
-    for step in NEAR:
-        landed([y_all[step]])
-        onward(step)
-
-    landed(branch_in)
-    for g in range(GROUPS):
-        span = slice(LANES * g, LANES * (g + 1))
-        out_ref[:, span] = (s.x[:, span].astype(F32) + s.bo[g].astype(F32)).astype(BF16)
     landed(border_xy)
-    packed = jnp.zeros((16, LANES), BF16)
-    total = jnp.zeros((CH, 1024), F32)
+    low = lane < 64
+    received = []
+    packed = jnp.zeros((16, LANES), F32)
     for i in range(4):
-        slot = lax.rem(at.xy - lax.div(nb_ref[at.tile, 7 - EDGE_DIRS[i]], NZ) + NXY, NXY)
-        total = total + dot(unfold(s.bgot[slot, i]), s.places[i])
-        slot = lax.rem(at.xy - lax.div(nb_ref[at.tile, 7 - CORNER_DIRS[i]], NZ) + NXY, NXY)
-        packed = jnp.where((lane >> 2) & 15 == i, s.bgot[slot, 4], packed)
-    total = total + dot(unfold(packed), s.places[4])
+        slot = lax.rem(at.xy - lax.div(nb_ref[7 - EDGE_DIRS[i], at.tile], NZ) + NXY, NXY)
+        received.append(s.bgot[slot, i].astype(F32))
+        slot = lax.rem(at.xy - lax.div(nb_ref[7 - CORNER_DIRS[i], at.tile], NZ) + NXY, NXY)
+        packed = jnp.where((lane >> 2) & 15 == i, s.bgot[slot, 4].astype(F32), packed)
+    total = dot(unfold(packed), s.places[2])
+    for pair in range(2):
+        one, two = received[2 * pair : 2 * pair + 2]
+        both = [jnp.where(low, one, roll(two, 64)), jnp.where(low, roll(one, 64), two)]
+        total = total + dot(jnp.concatenate(both, axis=0).astype(BF16), s.places[pair])
     for g in range(GROUPS):
         span = slice(LANES * g, LANES * (g + 1))
         gin_ref[:, span] = (s.acc[g] + total[:, span]).astype(BF16)
+
+    for step in NEAR[:2]:
+        landed([y_all[step]])
+        onward(step)
+    landed(taps_xy)
+    total = s.kown[2]
+    for k in range(1, NXY):
+        total = total + s.kxy[k]
+    s.kown[3] = total * SCALE
+    kall_ref[at.chan] = s.kown[3]
+    taps_all = [go(s.kown.at[3], kall_ref.at[at.chan], sem.kc, k, at.along_chan(k)) for k in range(1, NCHAN)]
+    for step in NEAR[2:]:
+        landed([y_all[step]])
+        onward(step)
 
     for step in (0, *NEAR):
         for k in (1, 3, 2):
@@ -628,11 +671,12 @@
 
 def body(inputs, grad_out, kernel, w_in, w_out, neighbours, rotations):
     vmem, semaphores = scratch_shapes()
-    tables = [pltpu.SMEM((NXY * NZ, 8), I32)] * 2
+    tables = [pltpu.SMEM((8, NXY * NZ), I32)] * 2
     scratch = [pltpu.SemaphoreType.DMA((7,)), *tables] + [pltpu.VMEM(shape, dtype) for shape, dtype in vmem.values()]
     for count in semaphores.values():
         scratch += [pltpu.SemaphoreType.DMA((count,))] * 2
     shapes = [((CH, 1024), BF16), ((CH, 1024), BF16), ((2, NX, NY, BLOCK, FULL), BF16), ((NCHAN, 8, LANES), F32)]
+    arrays = (neighbours.T, rotations.T, inputs.reshape(CH, 1024), grad_out.reshape(CH, 1024), kernel, w_in, w_out)
     results = pl.pallas_call(
         step_kernel,
         out_shape=[jax.ShapeDtypeStruct(shape, dtype) for shape, dtype in shapes],
@@ -641,7 +685,7 @@
         scratch_shapes=scratch,
         compiler_params=pltpu.CompilerParams(vmem_limit_bytes=50 << 20, collective_id=1, has_side_effects=True),
         name="step",
-    )(neighbours, rotations, inputs.reshape(CH, 1024), grad_out.reshape(CH, 1024), kernel, w_in, w_out)
+    )(*[pltpu.with_memory_space_constraint(array, pltpu.HBM) for array in arrays])
     shapes = [((CH, 1024), BF16), ((CH, 1024), BF16), ((FULL, HID), F32), ((HID, FULL), F32), ((TAPS, FULL), F32)]
     outputs, grad_in, grad_w_in, grad_w_out, grad_kernel = pl.pallas_call(
         last_kernel,

time: 89.4 us -> 84 us (0.940)
  local copies, waits for them, and re-layouts: 4.52 us -> 0 us
    unnamed x12 -> x0, local copies, waits for them, and re-layouts: 4.52 us -> none
where the time goes in v3:
time: 84 us; the launch traced here: 83.8 us
  Pallas kernels  83.2 us (99%)
    pallas_call x1, Pallas kernels, body(): pl.pallas_call(step_kernel, out_shape=[jax.ShapeDtypeStruct(shape, dtype)...  81.8 us

profile of v3, /device:TPU:1, one launch (start us, length us, event | category | flops | bytes accessed | tf_op | source)
XLA Modules:
  0.0 83.8 jit_solution(10322158991038084364)
XLA Ops:
  0.6 81.8 %step.1 = (bf16[32,1024]{1,0:T(8,128)(2,1)S(1)}, bf16[32,1024]{1,0:T(8,128)(2,1)S(1)}, bf16[2,4,8,32,256]{4,3,2,1,0:T(8,128)(2,1)S(1)}, f32[8,8,128]{2,1,0:T(8,128)S(1)}) custom-call(s32[8,96]{1,0:T(8,128)} %bitcast.8, s32[8,96]{1,0:T(8,128)} %bitcast.9, bf16[32,1024]{1,0:T(8,128)(2,1)} %bitcast.6, bf16[32,1024]{1,0:T(8,128)(2,1)} %bitcast.7, ...), custom_call_target="tpu_custom_call" | custom-call | tf_op jit(solution)/shard_map/step/pallas_call | solution.py:680
  82.4 1.4 %last.1 = (bf16[32,1024]{1,0:T(8,128)(2,1)}, bf16[32,1024]{1,0:T(8,128)(2,1)}, f32[256,1024]{1,0:T(8,128)}, f32[1024,256]{1,0:T(8,128)}, f32[25,256]{1,0:T(8,128)}) custom-call(bf16[32,1024]{1,0:T(8,128)(2,1)S(1)} %get-tuple-element.14.out_ref, bf16[32,1024]{1,0:T(8,128)(2,1)S(1)} %get-tuple-element.15.gin_ref, ...), custom_call_target="tpu_custom_call" | custom-call | tf_op jit(solution)/shard_map/last/pallas_call | solution.py:690

commit v4 on v3

--- a/solution.py
+++ b/solution.py
@@ -355,7 +355,7 @@
 Z_STEPS = (0, 1, 2, 11)
 BLOCK = 32
 NEAR = (1, 7, 2, 6, 3, 5, 4)
-FAR = (4, 3, 5, 2, 6, 1, 7, 0)
+PAIRS = (2, 1, 3, 0)
 
 
 def scratch_shapes():
@@ -371,13 +371,13 @@
         border=((5, *tile), BF16), bz=((NZ, 5, *tile), BF16), bout=((NXY, 5, *tile), BF16), bgot=((NXY, 5, *tile), BF16),
         kown=((4, 8, LANES), F32), kz=((6, 8, LANES), F32), kxy=((NXY, 8, LANES), F32),
         grads=((2, NX, FULL, FULL), F32), terms=((2, NX, FULL, FULL), BF16), rcore=((NX, FULL, FULL), BF16),
-        sx=((FULL, FULL), F32), tx=((NX, FULL, FULL), BF16), rx=((NX, NY, BLOCK, FULL), BF16),
-        sy=((BLOCK, FULL), F32), ty=((NY, BLOCK, FULL), BF16), ry=((NY, BLOCK, FULL), BF16),
+        sx=((FULL, FULL), F32), tx=((NX, FULL, FULL), BF16), rx=((NX, 4, 2 * BLOCK, FULL), BF16),
+        sp=((2 * BLOCK, FULL), F32), ty=((4, 2 * BLOCK, FULL), BF16), ry=((NY, BLOCK, FULL), BF16),
         tz=((BLOCK, FULL), BF16), uz=((BLOCK, FULL), BF16), rz=((7, BLOCK, FULL), BF16),
     )
     sems = dict(
-        z=NZ, cot=NCHAN, xy=NXY, s1=NCHAN, s2a=NCHAN, s2b=NCHAN, core=NX, x=NX * NY, y=NY, sz=6, bz=NZ, bxy=NXY,
-        kz=6, kxy=NXY, kc=NCHAN, ay=NY, ax=NX * NY, ac=NX * NY,
+        z=NZ, cot=NCHAN, xy=NXY, s1=NCHAN, s2a=NCHAN, s2b=NCHAN, core=NX, x=NX * 4, y=NY, sz=6, bz=NZ, bxy=NXY,
+        kz=6, kxy=NXY, kc=NCHAN, ay=NY, ax=NX * NY, ac=NX,
     )
     return vmem, sems
 
@@ -516,6 +516,10 @@
 
     landed(core_in)
     x_in = {}
+
+    def rows_of(q):
+        return pl.ds(pl.multiple_of(lax.rem(lax.div(at.y, 2) + q, 4) * 2 * BLOCK, 2 * BLOCK), 2 * BLOCK)
+
     for k in (2, 1, 3, 0):
         part = lax.rem(at.x + k, NX)
         total = s.grads[at.core, part] + s.rcore[part].astype(F32)
@@ -523,9 +527,8 @@
             s.sx[...] = total
             continue
         s.tx[k] = total.astype(BF16)
-        for step in FAR:
-            rows = pl.ds(pl.multiple_of(lax.rem(at.y + step, NY) * BLOCK, BLOCK), BLOCK)
-            x_in[k, step] = go(s.tx.at[k, rows], s.rx.at[k, step], sem.x, k * NY + step, at.along_x(k))
+        for q in PAIRS:
+            x_in[k, q] = go(s.tx.at[k, rows_of(q)], s.rx.at[k, q], sem.x, k * 4 + q, at.along_x(k))
 
     landed(grad_in)
     outer_spread(s.gh, s.kb, s.border)
@@ -533,17 +536,20 @@
     inner_spread(s.gh, s.go, s.kb, s.gb, s.acc)
     then_along_z(far, border_in, s.bz, sem.bz)
 
-    y_in = {}
-    for step in FAR:
-        landed([x_in[k, step] for k in (1, 3, 2)])
-        total = s.sx[pl.ds(pl.multiple_of(lax.rem(at.y + step, NY) * BLOCK, BLOCK), BLOCK)]
+    y_in = []
+    odd = lax.rem(at.y, 2)
+    for q in PAIRS:
+        landed([x_in[k, q] for k in (1, 3, 2)])
+        total = s.sx[rows_of(q)]
         for k in range(1, NX):
-            total = total + s.rx[k, step].astype(F32)
-        if step == 0:
-            s.sy[...] = total
-            continue
-        s.ty[step] = total.astype(BF16)
-        y_in[step] = go(s.ty.at[step], s.ry.at[step], sem.y, step, at.along_y(step))
+            total = total + s.rx[k, q].astype(F32)
+        s.ty[q] = total.astype(BF16)
+        if q == 0:
+            s.sp[...] = total
+        for e in (0, 1) if q else (1 - odd,):
+            step = lax.rem(lax.rem(lax.div(at.y, 2) + q, 4) * 2 + e - at.y + NY, NY)
+            half = pl.ds(pl.multiple_of(e * BLOCK, BLOCK), BLOCK)
+            y_in.append(go(s.ty.at[q, half], s.ry.at[step], sem.y, step, at.along_y(step)))
 
     s.kown[0] = tap_sums(s.pb, s.gb, s.ka)
     taps_far = [go(s.kown.at[0], s.kz.at[j], sem.kz, j, at.along_z(4 * j)) for j in (1, 2)]
@@ -553,8 +559,8 @@
         span = slice(LANES * g, LANES * (g + 1))
         out_ref[:, span] = (s.x[:, span].astype(F32) + s.bo[g].astype(F32)).astype(BF16)
 
-    landed([y_in[step] for step in NEAR])
-    total = s.sy[...]
+    landed(y_in)
+    total = s.sp[pl.ds(pl.multiple_of(odd * BLOCK, BLOCK), BLOCK)]
     for step in range(1, NY):
         total = total + s.ry[step].astype(F32)
     s.tz[...] = total.astype(BF16)
@@ -603,10 +609,28 @@
         block = all_ref.at[at.core, at.x, lax.rem(at.y - step + NY, NY)]
         for k in (2, 1, 3):
             x_all[k, step] = go(block, block, sem.ax, k * NY + step, at.along_x(k))
-        core_all.append(go(block, block, sem.ac, step, at.partner()))
 
     onward(0)
 
+    for step in NEAR[:2]:
+        landed([y_all[step]])
+        onward(step)
+    landed(taps_xy)
+    total = s.kown[2]
+    for k in range(1, NXY):
+        total = total + s.kxy[k]
+    s.kown[3] = total * SCALE
+    kall_ref[at.chan] = s.kown[3]
+    taps_all = [go(s.kown.at[3], kall_ref.at[at.chan], sem.kc, k, at.along_chan(k)) for k in range(1, NCHAN)]
+    for step in NEAR[2:]:
+        landed([y_all[step]])
+        onward(step)
+
+    for k in (0, 1, 3, 2):
+        if k:
+            landed([x_all[k, step] for step in (0, *NEAR)])
+        row = all_ref.at[at.core, lax.rem(at.x - k + NX, NX)]
+        core_all.append(go(row, row, sem.ac, k, at.partner()))
     landed(border_xy)
     low = lane < 64
     received = []
@@ -624,26 +648,6 @@
     for g in range(GROUPS):
         span = slice(LANES * g, LANES * (g + 1))
         gin_ref[:, span] = (s.acc[g] + total[:, span]).astype(BF16)
-
-    for step in NEAR[:2]:
-        landed([y_all[step]])
-        onward(step)
-    landed(taps_xy)
-    total = s.kown[2]
-    for k in range(1, NXY):
-        total = total + s.kxy[k]
-    s.kown[3] = total * SCALE
-    kall_ref[at.chan] = s.kown[3]
-    taps_all = [go(s.kown.at[3], kall_ref.at[at.chan], sem.kc, k, at.along_chan(k)) for k in range(1, NCHAN)]
-    for step in NEAR[2:]:
-        landed([y_all[step]])
-        onward(step)
-
-    for step in (0, *NEAR):
-        for k in (1, 3, 2):
-            landed([x_all[k, step]])
-            block = all_ref.at[at.core, lax.rem(at.x - k + NX, NX), lax.rem(at.y - step + NY, NY)]
-            core_all.append(go(block, block, sem.ac, k * NY + step, at.partner()))
     landed(taps_all)
     landed(core_all)
     for copy in copies:

time: 84 us -> 83 us (0.988)
  Pallas kernels: 83.2 us -> 82.2 us
    pallas_call x1, Pallas kernels: 81.8 us -> 80.8 us  [body(): pl.pallas_call(step_kernel, out_shape=[jax.ShapeDtypeStruct(shape, dtype)...]
where the time goes in v4:
time: 83 us; the launch traced here: 82.8 us
  Pallas kernels  82.2 us (99%)
    pallas_call x1, Pallas kernels, body(): pl.pallas_call(step_kernel, out_shape=[jax.ShapeDtypeStruct(shape, dtype)...  80.8 us

profile of v4, /device:TPU:1, one launch (start us, length us, event | category | flops | bytes accessed | tf_op | source)
XLA Modules:
  0.0 82.8 jit_solution(14438451273390190126)
XLA Ops:
  0.6 80.8 %step.1 = (bf16[32,1024]{1,0:T(8,128)(2,1)S(1)}, bf16[32,1024]{1,0:T(8,128)(2,1)S(1)}, bf16[2,4,8,32,256]{4,3,2,1,0:T(8,128)(2,1)S(1)}, f32[8,8,128]{2,1,0:T(8,128)S(1)}) custom-call(s32[8,96]{1,0:T(8,128)} %bitcast.8, s32[8,96]{1,0:T(8,128)} %bitcast.9, bf16[32,1024]{1,0:T(8,128)(2,1)} %bitcast.6, bf16[32,1024]{1,0:T(8,128)(2,1)} %bitcast.7, ...), custom_call_target="tpu_custom_call" | custom-call | tf_op jit(solution)/shard_map/step/pallas_call | solution.py:684
  81.4 1.4 %last.1 = (bf16[32,1024]{1,0:T(8,128)(2,1)}, bf16[32,1024]{1,0:T(8,128)(2,1)}, f32[256,1024]{1,0:T(8,128)}, f32[1024,256]{1,0:T(8,128)}, f32[25,256]{1,0:T(8,128)}) custom-call(bf16[32,1024]{1,0:T(8,128)(2,1)S(1)} %get-tuple-element.14.out_ref, bf16[32,1024]{1,0:T(8,128)(2,1)S(1)} %get-tuple-element.15.gin_ref, ...), custom_call_target="tpu_custom_call" | custom-call | tf_op jit(solution)/shard_map/last/pallas_call | solution.py:694

commit v5 on v4

--- a/solution.py
+++ b/solution.py
@@ -615,6 +615,10 @@
     for step in NEAR[:2]:
         landed([y_all[step]])
         onward(step)
+    for step in NEAR[2:]:
+        landed([y_all[step]])
+        onward(step)
+
     landed(taps_xy)
     total = s.kown[2]
     for k in range(1, NXY):
@@ -622,10 +626,6 @@
     s.kown[3] = total * SCALE
     kall_ref[at.chan] = s.kown[3]
     taps_all = [go(s.kown.at[3], kall_ref.at[at.chan], sem.kc, k, at.along_chan(k)) for k in range(1, NCHAN)]
-    for step in NEAR[2:]:
-        landed([y_all[step]])
-        onward(step)
-
     for k in (0, 1, 3, 2):
         if k:
             landed([x_all[k, step] for step in (0, *NEAR)])

time: 83 us -> 82.9 us (level)
  no operation moved by 1% of the time
where the time goes in v5:
time: 82.9 us
  Pallas kernels  82.2 us (99%)
    pallas_call x1, Pallas kernels, body(): pl.pallas_call(step_kernel, out_shape=[jax.ShapeDtypeStruct(shape, dtype)...  80.8 us

profile of v5, /device:TPU:1, one launch (start us, length us, event | category | flops | bytes accessed | tf_op | source)
XLA Modules:
  0.0 82.9 jit_solution(12569459759590131426)
XLA Ops:
  0.6 80.8 %step.1 = (bf16[32,1024]{1,0:T(8,128)(2,1)S(1)}, bf16[32,1024]{1,0:T(8,128)(2,1)S(1)}, bf16[2,4,8,32,256]{4,3,2,1,0:T(8,128)(2,1)S(1)}, f32[8,8,128]{2,1,0:T(8,128)S(1)}) custom-call(s32[8,96]{1,0:T(8,128)} %bitcast.8, s32[8,96]{1,0:T(8,128)} %bitcast.9, bf16[32,1024]{1,0:T(8,128)(2,1)} %bitcast.6, bf16[32,1024]{1,0:T(8,128)(2,1)} %bitcast.7, ...), custom_call_target="tpu_custom_call" | custom-call | tf_op jit(solution)/shard_map/step/pallas_call | solution.py:684
  81.4 1.4 %last.1 = (bf16[32,1024]{1,0:T(8,128)(2,1)}, bf16[32,1024]{1,0:T(8,128)(2,1)}, f32[256,1024]{1,0:T(8,128)}, f32[1024,256]{1,0:T(8,128)}, f32[25,256]{1,0:T(8,128)}) custom-call(bf16[32,1024]{1,0:T(8,128)(2,1)S(1)} %get-tuple-element.14.out_ref, bf16[32,1024]{1,0:T(8,128)(2,1)S(1)} %get-tuple-element.15.gin_ref, ...), custom_call_target="tpu_custom_call" | custom-call | tf_op jit(solution)/shard_map/last/pallas_call | solution.py:694
